TPU v7x, 512 devices: a whole 4x4x16 slice. The times are simulated.
512 devices in a mesh: expert: 32 (over z_hi, x, core), row: 4 (over z_lo), col: 4 (over y).
Axes of the slice: x: 4, y: 4, z: 16 (z_hi: 4, z_lo: 4; z = z_hi * 4 + z_lo), core: 2. Of those that a mesh axis runs over, the one named last changes fastest.
Arguments:
- tokens: bfloat16 [32768, 3584], P(('expert', 'col'), 'row'), may hold values from -6 to 6
- slots: int32 [128, 6, 32, 2], P(('expert', 'col')), may hold values from 0 to 255
- counts: int32 [6, 32], replicated, may hold values from 1 to 256, as said below
- owner: int32 [32], replicated, may hold values from 0 to 31, each once
Outputs:
- moments: float32 [32, 3584, 3584], P('expert', 'row', 'col')
Inputs may be any that keep to these rules, and one draw needn't show every extreme that they name: `counts`: in every panel at least one expert's count is 256.
All inputs are finite; a program needn't handle non-finite values.
Results may differ from a plain program's by a relative error of at most 0.0003.
Values may be sent and summed in bfloat16 or wider, within the bound.
No kernel may reach another device: no remote copies, remote signals or barrier semaphores. Data moves between devices by JAX's collectives and lax.ppermute only.
A program may use at most 64 MiB of HBM per device.

v0:
```python
import jax
import jax.numpy as jnp
from jax import lax
from jax.sharding import PartitionSpec as P

SIDE = 4
SEGMENTS = 4
CHIPS = 8


def swap(rows, axis, mask):
    return lax.ppermute(rows, axis, [(i, i ^ mask) for i in range(SIDE)])


def routed_rows(tokens, slots, counts, owner):
    groups = owner.shape[0]
    panels, slot_count = slots.shape[1], slots.shape[3]
    block = lax.axis_index("expert") * lax.axis_size("col") + lax.axis_index("col")
    place = jnp.arange(groups, dtype=jnp.int32)
    segment = lax.axis_index("expert") // CHIPS
    group = ((place % SEGMENTS) ^ segment) * CHIPS + place // SEGMENTS
    mine = (owner[None, :] == group[:, None]).astype(jnp.float32)
    position = block * slot_count + jnp.arange(slot_count, dtype=jnp.int32)
    usable = position[None, None, :] < counts[:, :, None]
    table = jnp.where(usable, slots[0], -1).astype(jnp.float32)
    table = jnp.transpose(table, (1, 0, 2)).reshape(groups, panels * slot_count)
    picks = jnp.dot(mine, table, precision=lax.Precision.HIGHEST).astype(jnp.int32)
    hot = picks.reshape(-1, 1) == jnp.arange(tokens.shape[0], dtype=jnp.int32)[None, :]
    rows = jnp.dot(hot.astype(tokens.dtype), tokens, preferred_element_type=jnp.float32).astype(tokens.dtype)
    totals = jnp.sum(jnp.where(owner == lax.axis_index("expert"), counts, 0)).astype(jnp.float32)
    return rows.reshape(groups, panels * slot_count, tokens.shape[1]), totals


def moment_parts(rows):
    lefts = [rows] + [swap(rows, "col", m) for m in (1, 3, 2)]
    far = swap(rows, "row", 2)
    near = swap(rows, "row", 1)
    features = [rows, near, far, swap(far, "row", 1)]
    here = lax.axis_index("row") ^ lax.axis_index("col")
    picked = [pick(features, here ^ m) for m in (0, 1, 3, 2)]
    rights = [picked[0]] + [swap(q, "col", m) for q, m in zip(picked[1:], (1, 3, 2))]
    return list(zip(lefts, rights))


def pick(choices, index):
    chosen = choices[0]
    for i in range(1, len(choices)):
        chosen = jnp.where(index == i, choices[i], chosen)
    return chosen


def reach(rows, d):
    return lax.ppermute(rows, "expert", [(e, e ^ (d * CHIPS)) for e in range(SEGMENTS * CHIPS)])


def per_device(tokens, slots, counts, owner):
  outgoing, total = routed_rows(tokens, slots, counts, owner)
  width = tokens.shape[1]
  near_groups = [[z * CHIPS + i for i in range(CHIPS)] for z in range(SEGMENTS)]
  mixed = lax.all_to_all(outgoing.reshape(CHIPS, -1, width), "expert", 0, 0, tiled=True, axis_index_groups=near_groups)
  each = mixed.shape[1] // SEGMENTS
  pieces = [mixed[:, d * each : (d + 1) * each].reshape(-1, width) for d in range(SEGMENTS)]
  pieces = [pieces[0]] + [reach(pieces[d], d) for d in range(1, SEGMENTS)]
  tile = None
  for group in ((0, 1), (3, 2)):
      part = jnp.concatenate([pieces[d] for d in group])
      for left, right in moment_parts(part):
          term = lax.dot_general(left, right, (((0,), (0,)), ((), ())), preferred_element_type=jnp.float32)
          tile = term if tile is None else tile + term
  return (tile / total)[None]


def solution(mesh):
    return jax.shard_map(
        per_device,
        mesh=mesh,
        in_specs=(P(("expert", "col"), "row"), P(("expert", "col"), None, None, None), P(), P()),
        out_specs=P("expert", "row", "col"),
        check_vma=False,
    )
```

profile of v0, /device:TPU:1, one launch (start us, length us, event | category | flops | bytes accessed | tf_op | source)
XLA Modules:
  0.0 169.7 jit_solution(7288158527439893921)
XLA Ops:
  0.0 0.8 fusion.18
  0.9 0.8 convolution_convert_fusion.1
  1.8 0.1 eq.87
  1.9 0.4 convolution_convert_fusion
  2.4 20.4 %all_to_all.5 = bf16[8,48,896]{2,1,0:T(8,128)(2,1)S(1)} all-to-all(bf16[8,48,896]{2,1,0:T(8,128)(2,1)S(1)} %bitcast.25), channel_id=1, replica_groups={{0,16,32,48,64,80,96,112},{128,144,160,176,192,208,224,240},{256,272,28..., dimensions={0} | all-to-all | bytes 1376256 | tf_op jit(solution)/shard_map/all_to_all | solution.py:60
  22.8 0.1 fusion.22
  23.0 5.2 %collective-permute-start = (bf16[96,896]{1,0:T(8,128)(2,1)S(1)}, bf16[96,896]{1,0:T(8,128)(2,1)S(1)}, u32[]{:S(2)}, u32[]{:S(2)}) collective-permute-start(bf16[96,896]{1,0:T(8,128)(2,1)S(1)} %reshape.48), channel_id=1, source_target_pairs={{0,128},{16,144},{32,160},{48,176},{64,192},{80,208},{96,224},{112... | collective-permute-start | bytes 516104 | tf_op jit(solution)/shard_map/ppermute | solution.py:53
  28.3 8.8 %collective-permute-start.10 = (bf16[96,896]{1,0:T(8,128)(2,1)S(1)}, bf16[96,896]{1,0:T(8,128)(2,1)S(1)}, u32[]{:S(2)}, u32[]{:S(2)}) collective-permute-start(bf16[96,896]{1,0:T(8,128)(2,1)S(1)} %reshape.49), channel_id=1, source_target_pairs={{0,384},{16,400},{32,416},{48,432},{64,448},{80,464},{96,480},{112... | collective-permute-start | bytes 516104 | tf_op jit(solution)/shard_map/ppermute | solution.py:53
  37.1 8.4 %collective-permute-done = bf16[96,896]{1,0:T(8,128)(2,1)S(1)} collective-permute-done((bf16[96,896]{1,0:T(8,128)(2,1)S(1)}, bf16[96,896]{1,0:T(8,128)(2,1)S(1)}, u32[]{:S(2)}, u32[]{:S(2)}) %collective-permute-start) | collective-permute-done | bytes 172064 | tf_op jit(solution)/shard_map/ppermute | solution.py:53
  45.5 1.9 %collective-permute-start.1 = (bf16[192,896]{1,0:T(8,128)(2,1)S(1)}, bf16[192,896]{1,0:T(8,128)(2,1)S(1)}, u32[]{:S(2)}, u32[]{:S(2)}) collective-permute-start(bf16[192,896]{1,0:T(8,128)(2,1)S(1)} %constant_dynamic-update-slice_fusion), channel_id=1, source_target_pairs={{0,8},{4,12},{8,0},{12,4},{1,9},{5,13},{9,1},{13,5},{2,10},{6,14},... | collective-permute-start | bytes 1032200 | tf_op jit(solution)/shard_map/ppermute | solution.py:12
  47.5 12.3 %collective-permute-start.11 = (bf16[96,896]{1,0:T(8,128)(2,1)S(1)}, bf16[96,896]{1,0:T(8,128)(2,1)S(1)}, u32[]{:S(2)}, u32[]{:S(2)}) collective-permute-start(bf16[96,896]{1,0:T(8,128)(2,1)S(1)} %reshape.50), channel_id=1, source_target_pairs={{0,256},{16,272},{32,288},{48,304},{64,320},{80,336},{96,352},{112... | collective-permute-start | bytes 516104 | tf_op jit(solution)/shard_map/ppermute | solution.py:53
  59.9 1.9 %collective-permute-start.3 = (bf16[192,896]{1,0:T(8,128)(2,1)S(1)}, bf16[192,896]{1,0:T(8,128)(2,1)S(1)}, u32[]{:S(2)}, u32[]{:S(2)}) collective-permute-start(bf16[192,896]{1,0:T(8,128)(2,1)S(1)} %constant_dynamic-update-slice_fusion), channel_id=1, source_target_pairs={{0,4},{4,0},{8,12},{12,8},{1,5},{5,1},{9,13},{13,9},{2,6},{6,2},{1... | collective-permute-start | bytes 1032200 | tf_op jit(solution)/shard_map/ppermute | solution.py:12
  61.8 19.7 %collective-permute-done.11 = bf16[96,896]{1,0:T(8,128)(2,1)S(1)} collective-permute-done((bf16[96,896]{1,0:T(8,128)(2,1)S(1)}, bf16[96,896]{1,0:T(8,128)(2,1)S(1)}, u32[]{:S(2)}, u32[]{:S(2)}) %collective-permute-start.11) | collective-permute-done | bytes 172064 | tf_op jit(solution)/shard_map/ppermute | solution.py:53
  81.5 1.9 %collective-permute-start.12 = (bf16[192,896]{1,0:T(8,128)(2,1)S(1)}, bf16[192,896]{1,0:T(8,128)(2,1)S(1)}, u32[]{:S(2)}, u32[]{:S(2)}) collective-permute-start(bf16[192,896]{1,0:T(8,128)(2,1)S(1)} %constant_dynamic-update-slice_fusion.2), channel_id=1, source_target_pairs={{0,8},{4,12},{8,0},{12,4},{1,9},{5,13},{9,1},{13,5},{2,10},{6,14},... | collective-permute-start | bytes 1032200 | tf_op jit(solution)/shard_map/ppermute | solution.py:12
  83.5 1.9 %collective-permute-start.2 = (bf16[192,896]{1,0:T(8,128)(2,1)S(1)}, bf16[192,896]{1,0:T(8,128)(2,1)S(1)}, u32[]{:S(2)}, u32[]{:S(2)}) collective-permute-start(bf16[192,896]{1,0:T(8,128)(2,1)S(1)} %collective-permute-done.1), channel_id=1, source_target_pairs={{0,4},{4,0},{8,12},{12,8},{1,5},{5,1},{9,13},{13,9},{2,6},{6,2},{1... | collective-permute-start | bytes 1032200 | tf_op jit(solution)/shard_map/ppermute | solution.py:12
  85.5 0.6 select_reduce_fusion
  86.8 3.2 %collective-permute-start.6 = (bf16[192,896]{1,0:T(8,128)(2,1)S(1)}, bf16[192,896]{1,0:T(8,128)(2,1)S(1)}, u32[]{:S(2)}, u32[]{:S(2)}) collective-permute-start(bf16[192,896]{1,0:T(8,128)(2,1)S(1)} %constant_dynamic-update-slice_fusion), channel_id=1, source_target_pairs={{0,3},{1,2},{2,1},{3,0},{4,7},{5,6},{6,5},{7,4},{8,11},{9,10},{10,... | collective-permute-start | bytes 1032200 | tf_op jit(solution)/shard_map/ppermute | solution.py:12
  89.9 1.9 %collective-permute-start.4 = (bf16[192,896]{1,0:T(8,128)(2,1)S(1)}, bf16[192,896]{1,0:T(8,128)(2,1)S(1)}, u32[]{:S(2)}, u32[]{:S(2)}) collective-permute-start(bf16[192,896]{1,0:T(8,128)(2,1)S(1)} %constant_dynamic-update-slice_fusion), channel_id=1, source_target_pairs={{0,1},{1,0},{2,3},{3,2},{4,5},{5,4},{6,7},{7,6},{8,9},{9,8},{10,11... | collective-permute-start | bytes 1032200 | tf_op jit(solution)/shard_map/ppermute | solution.py:12
  91.9 2.8 %collective-permute-start.14 = (bf16[192,896]{1,0:T(8,128)(2,1)S(1)}, bf16[192,896]{1,0:T(8,128)(2,1)S(1)}, u32[]{:S(2)}, u32[]{:S(2)}) collective-permute-start(bf16[192,896]{1,0:T(8,128)(2,1)S(1)} %constant_dynamic-update-slice_fusion.2), channel_id=1, source_target_pairs={{0,4},{4,0},{8,12},{12,8},{1,5},{5,1},{9,13},{13,9},{2,6},{6,2},{1... | collective-permute-start | bytes 1032200 | tf_op jit(solution)/shard_map/ppermute | solution.py:12
  94.7 3.7 %collective-permute-done.12 = bf16[192,896]{1,0:T(8,128)(2,1)S(1)} collective-permute-done((bf16[192,896]{1,0:T(8,128)(2,1)S(1)}, bf16[192,896]{1,0:T(8,128)(2,1)S(1)}, u32[]{:S(2)}, u32[]{:S(2)}) %collective-permute-start.12) | collective-permute-done | bytes 344096 | tf_op jit(solution)/shard_map/ppermute | solution.py:12
  98.4 1.9 %collective-permute-start.13 = (bf16[192,896]{1,0:T(8,128)(2,1)S(1)}, bf16[192,896]{1,0:T(8,128)(2,1)S(1)}, u32[]{:S(2)}, u32[]{:S(2)}) collective-permute-start(bf16[192,896]{1,0:T(8,128)(2,1)S(1)} %collective-permute-done.12), channel_id=1, source_target_pairs={{0,4},{4,0},{8,12},{12,8},{1,5},{5,1},{9,13},{13,9},{2,6},{6,2},{1... | collective-permute-start | bytes 1032200 | tf_op jit(solution)/shard_map/ppermute | solution.py:12
  100.3 2.9 %collective-permute-done.2 = bf16[192,896]{1,0:T(8,128)(2,1)S(1)} collective-permute-done((bf16[192,896]{1,0:T(8,128)(2,1)S(1)}, bf16[192,896]{1,0:T(8,128)(2,1)S(1)}, u32[]{:S(2)}, u32[]{:S(2)}) %collective-permute-start.2) | collective-permute-done | bytes 344096 | tf_op jit(solution)/shard_map/ppermute | solution.py:12
  103.2 0.2 select_select_fusion.5
  103.4 3.4 %collective-permute-start.7 = (bf16[192,896]{1,0:T(8,128)(2,1)S(1)}, bf16[192,896]{1,0:T(8,128)(2,1)S(1)}, u32[]{:S(2)}, u32[]{:S(2)}) collective-permute-start(bf16[192,896]{1,0:T(8,128)(2,1)S(1)} %get-tuple-element.7), channel_id=1, source_target_pairs={{0,3},{1,2},{2,1},{3,0},{4,7},{5,6},{6,5},{7,4},{8,11},{9,10},{10,... | collective-permute-start | bytes 1032200 | tf_op jit(solution)/shard_map/ppermute | solution.py:12
  106.8 0.7 fusion.3
  107.4 3.1 %collective-permute-done.14 = bf16[192,896]{1,0:T(8,128)(2,1)S(1)} collective-permute-done((bf16[192,896]{1,0:T(8,128)(2,1)S(1)}, bf16[192,896]{1,0:T(8,128)(2,1)S(1)}, u32[]{:S(2)}, u32[]{:S(2)}) %collective-permute-start.14) | collective-permute-done | bytes 344096 | tf_op jit(solution)/shard_map/ppermute | solution.py:12
  110.6 3.6 %collective-permute-start.8 = (bf16[192,896]{1,0:T(8,128)(2,1)S(1)}, bf16[192,896]{1,0:T(8,128)(2,1)S(1)}, u32[]{:S(2)}, u32[]{:S(2)}) collective-permute-start(bf16[192,896]{1,0:T(8,128)(2,1)S(1)} %constant_dynamic-update-slice_fusion), channel_id=1, source_target_pairs={{0,2},{1,3},{2,0},{3,1},{4,6},{5,7},{6,4},{7,5},{8,10},{9,11},{10,... | collective-permute-start | bytes 1032200 | tf_op jit(solution)/shard_map/ppermute | solution.py:12
  114.1 3.8 %collective-permute-done.13 = bf16[192,896]{1,0:T(8,128)(2,1)S(1)} collective-permute-done((bf16[192,896]{1,0:T(8,128)(2,1)S(1)}, bf16[192,896]{1,0:T(8,128)(2,1)S(1)}, u32[]{:S(2)}, u32[]{:S(2)}) %collective-permute-start.13) | collective-permute-done | bytes 344096 | tf_op jit(solution)/shard_map/ppermute | solution.py:12
  117.9 3.6 %collective-permute-start.9 = (bf16[192,896]{1,0:T(8,128)(2,1)S(1)}, bf16[192,896]{1,0:T(8,128)(2,1)S(1)}, u32[]{:S(2)}, u32[]{:S(2)}) collective-permute-start(bf16[192,896]{1,0:T(8,128)(2,1)S(1)} %get-tuple-element.6), channel_id=1, source_target_pairs={{0,2},{1,3},{2,0},{3,1},{4,6},{5,7},{6,4},{7,5},{8,10},{9,11},{10,... | collective-permute-start | bytes 1032200 | tf_op jit(solution)/shard_map/ppermute | solution.py:12
  121.5 0.2 select_select_fusion.2
  121.7 2.7 %collective-permute-start.17 = (bf16[192,896]{1,0:T(8,128)(2,1)S(1)}, bf16[192,896]{1,0:T(8,128)(2,1)S(1)}, u32[]{:S(2)}, u32[]{:S(2)}) collective-permute-start(bf16[192,896]{1,0:T(8,128)(2,1)S(1)} %constant_dynamic-update-slice_fusion.2), channel_id=1, source_target_pairs={{0,3},{1,2},{2,1},{3,0},{4,7},{5,6},{6,5},{7,4},{8,11},{9,10},{10,... | collective-permute-start | bytes 1032200 | tf_op jit(solution)/shard_map/ppermute | solution.py:12
  124.4 2.1 %collective-permute-start.5 = (bf16[192,896]{1,0:T(8,128)(2,1)S(1)}, bf16[192,896]{1,0:T(8,128)(2,1)S(1)}, u32[]{:S(2)}, u32[]{:S(2)}) collective-permute-start(bf16[192,896]{1,0:T(8,128)(2,1)S(1)} %get-tuple-element.5), channel_id=1, source_target_pairs={{0,1},{1,0},{2,3},{3,2},{4,5},{5,4},{6,7},{7,6},{8,9},{9,8},{10,11... | collective-permute-start | bytes 1032200 | tf_op jit(solution)/shard_map/ppermute | solution.py:12
  126.5 0.7 fusion.24
  127.2 3.2 %collective-permute-start.15 = (bf16[192,896]{1,0:T(8,128)(2,1)S(1)}, bf16[192,896]{1,0:T(8,128)(2,1)S(1)}, u32[]{:S(2)}, u32[]{:S(2)}) collective-permute-start(bf16[192,896]{1,0:T(8,128)(2,1)S(1)} %constant_dynamic-update-slice_fusion.2), channel_id=1, source_target_pairs={{0,1},{1,0},{2,3},{3,2},{4,5},{5,4},{6,7},{7,6},{8,9},{9,8},{10,11... | collective-permute-start | bytes 1032200 | tf_op jit(solution)/shard_map/ppermute | solution.py:12
  130.4 3.8 %collective-permute-start.18 = (bf16[192,896]{1,0:T(8,128)(2,1)S(1)}, bf16[192,896]{1,0:T(8,128)(2,1)S(1)}, u32[]{:S(2)}, u32[]{:S(2)}) collective-permute-start(bf16[192,896]{1,0:T(8,128)(2,1)S(1)} %get-tuple-element.10), channel_id=1, source_target_pairs={{0,3},{1,2},{2,1},{3,0},{4,7},{5,6},{6,5},{7,4},{8,11},{9,10},{10,... | collective-permute-start | bytes 1032200 | tf_op jit(solution)/shard_map/ppermute | solution.py:12
  134.2 0.7 fusion.25
  134.9 2.0 %collective-permute-start.19 = (bf16[192,896]{1,0:T(8,128)(2,1)S(1)}, bf16[192,896]{1,0:T(8,128)(2,1)S(1)}, u32[]{:S(2)}, u32[]{:S(2)}) collective-permute-start(bf16[192,896]{1,0:T(8,128)(2,1)S(1)} %constant_dynamic-update-slice_fusion.2), channel_id=1, source_target_pairs={{0,2},{1,3},{2,0},{3,1},{4,6},{5,7},{6,4},{7,5},{8,10},{9,11},{10,... | collective-permute-start | bytes 1032200 | tf_op jit(solution)/shard_map/ppermute | solution.py:12
  136.9 4.8 %collective-permute-start.20 = (bf16[192,896]{1,0:T(8,128)(2,1)S(1)}, bf16[192,896]{1,0:T(8,128)(2,1)S(1)}, u32[]{:S(2)}, u32[]{:S(2)}) collective-permute-start(bf16[192,896]{1,0:T(8,128)(2,1)S(1)} %get-tuple-element.9), channel_id=1, source_target_pairs={{0,2},{1,3},{2,0},{3,1},{4,6},{5,7},{6,4},{7,5},{8,10},{9,11},{10,... | collective-permute-start | bytes 1032200 | tf_op jit(solution)/shard_map/ppermute | solution.py:12
  141.7 0.7 fusion.23
  142.4 1.9 %collective-permute-start.16 = (bf16[192,896]{1,0:T(8,128)(2,1)S(1)}, bf16[192,896]{1,0:T(8,128)(2,1)S(1)}, u32[]{:S(2)}, u32[]{:S(2)}) collective-permute-start(bf16[192,896]{1,0:T(8,128)(2,1)S(1)} %get-tuple-element.8), channel_id=1, source_target_pairs={{0,1},{1,0},{2,3},{3,2},{4,5},{5,4},{6,7},{7,6},{8,9},{9,8},{10,11... | collective-permute-start | bytes 1032200 | tf_op jit(solution)/shard_map/ppermute | solution.py:12
  144.3 2.4 %collective-permute-done.18 = bf16[192,896]{1,0:T(8,128)(2,1)S(1)} collective-permute-done((bf16[192,896]{1,0:T(8,128)(2,1)S(1)}, bf16[192,896]{1,0:T(8,128)(2,1)S(1)}, u32[]{:S(2)}, u32[]{:S(2)}) %collective-permute-start.18) | collective-permute-done | bytes 344096 | tf_op jit(solution)/shard_map/ppermute | solution.py:12
  146.7 0.7 fusion.27
  147.4 4.4 %collective-permute-done.19 = bf16[192,896]{1,0:T(8,128)(2,1)S(1)} collective-permute-done((bf16[192,896]{1,0:T(8,128)(2,1)S(1)}, bf16[192,896]{1,0:T(8,128)(2,1)S(1)}, u32[]{:S(2)}, u32[]{:S(2)}) %collective-permute-start.19) | collective-permute-done | bytes 344096 | tf_op jit(solution)/shard_map/ppermute | solution.py:12
  151.8 7.4 %collective-permute-done.20 = bf16[192,896]{1,0:T(8,128)(2,1)S(1)} collective-permute-done((bf16[192,896]{1,0:T(8,128)(2,1)S(1)}, bf16[192,896]{1,0:T(8,128)(2,1)S(1)}, u32[]{:S(2)}, u32[]{:S(2)}) %collective-permute-start.20) | collective-permute-done | bytes 344096 | tf_op jit(solution)/shard_map/ppermute | solution.py:12
  159.2 0.7 fusion.28
  159.9 6.0 %collective-permute-done.16 = bf16[192,896]{1,0:T(8,128)(2,1)S(1)} collective-permute-done((bf16[192,896]{1,0:T(8,128)(2,1)S(1)}, bf16[192,896]{1,0:T(8,128)(2,1)S(1)}, u32[]{:S(2)}, u32[]{:S(2)}) %collective-permute-start.16) | collective-permute-done | bytes 344096 | tf_op jit(solution)/shard_map/ppermute | solution.py:12
  165.9 0.7 fusion.26
  166.6 3.1 %divide_bitcast_fusion = f32[1,896,896]{2,1,0:T(8,128)} fusion(f32[896,896]{1,0:T(8,128)S(1)} %fusion.28, f32[896,896]{1,0:T(8,128)S(1)} %fusion.27, f32[896,896]{1,0:T(8,128)S(1)} %fusion.26, f32[896,896]{1,0:T(8,128)S(1)} %fusion.25, f32[896,896]{1,0:T(8,128)S(1)} %fusion.24, f32[896,896]{1,0:T(8,128)S(1)} %fusion.3, f32[896,896]{1,0:T(8,128)S(1)} %fusion.23, ...), kind=kOutput, calls=%fused_computation | convolution fusion | flops 315219968 | bytes 27066376 | tf_op jit(solution)/shard_map/dot_general | solution.py:68
  (30 shorter events, 0.4 us)
Async XLA Ops:
  0.0 1.9 %copy-start = (bf16[256,896]{1,0:T(8,128)(2,1)S(1)}, bf16[256,896]{1,0:T(8,128)(2,1)}, u32[]{:S(2)}) copy-start(bf16[256,896]{1,0:T(8,128)(2,1)} %param.4) | copy-start | bytes 1376260
  2.4 83.1 %copy-start.2 = (s32[32]{0:T(128)S(1)}, s32[32]{0:T(128)}, u32[]{:S(2)}) copy-start(s32[32]{0:T(128)} %param.7) | copy-start | bytes 388
  2.4 83.1 %copy-start.1 = (s32[6,32]{1,0:T(8,128)S(1)}, s32[6,32]{1,0:T(8,128)}, u32[]{:S(2)}) copy-start(s32[6,32]{1,0:T(8,128)} %param.6) | copy-start | bytes 2308
  23.0 22.5 %collective-permute-start = (bf16[96,896]{1,0:T(8,128)(2,1)S(1)}, bf16[96,896]{1,0:T(8,128)(2,1)S(1)}, u32[]{:S(2)}, u32[]{:S(2)}) collective-permute-start(bf16[96,896]{1,0:T(8,128)(2,1)S(1)} %reshape.48), channel_id=1, source_target_pairs={{0,128},{16,144},{32,160},{48,176},{64,192},{80,208},{96,224},{112... | collective-permute-start | bytes 516104 | tf_op jit(solution)/shard_map/ppermute | solution.py:53
  28.3 33.5 %collective-permute-start.10 = (bf16[96,896]{1,0:T(8,128)(2,1)S(1)}, bf16[96,896]{1,0:T(8,128)(2,1)S(1)}, u32[]{:S(2)}, u32[]{:S(2)}) collective-permute-start(bf16[96,896]{1,0:T(8,128)(2,1)S(1)} %reshape.49), channel_id=1, source_target_pairs={{0,384},{16,400},{32,416},{48,432},{64,448},{80,464},{96,480},{112... | collective-permute-start | bytes 516104 | tf_op jit(solution)/shard_map/ppermute | solution.py:53
  45.5 37.9 %collective-permute-start.1 = (bf16[192,896]{1,0:T(8,128)(2,1)S(1)}, bf16[192,896]{1,0:T(8,128)(2,1)S(1)}, u32[]{:S(2)}, u32[]{:S(2)}) collective-permute-start(bf16[192,896]{1,0:T(8,128)(2,1)S(1)} %constant_dynamic-update-slice_fusion), channel_id=1, source_target_pairs={{0,8},{4,12},{8,0},{12,4},{1,9},{5,13},{9,1},{13,5},{2,10},{6,14},... | collective-permute-start | bytes 1032200 | tf_op jit(solution)/shard_map/ppermute | solution.py:12
  47.5 34.0 %collective-permute-start.11 = (bf16[96,896]{1,0:T(8,128)(2,1)S(1)}, bf16[96,896]{1,0:T(8,128)(2,1)S(1)}, u32[]{:S(2)}, u32[]{:S(2)}) collective-permute-start(bf16[96,896]{1,0:T(8,128)(2,1)S(1)} %reshape.50), channel_id=1, source_target_pairs={{0,256},{16,272},{32,288},{48,304},{64,320},{80,336},{96,352},{112... | collective-permute-start | bytes 516104 | tf_op jit(solution)/shard_map/ppermute | solution.py:53
  59.9 32.0 %collective-permute-start.3 = (bf16[192,896]{1,0:T(8,128)(2,1)S(1)}, bf16[192,896]{1,0:T(8,128)(2,1)S(1)}, u32[]{:S(2)}, u32[]{:S(2)}) collective-permute-start(bf16[192,896]{1,0:T(8,128)(2,1)S(1)} %constant_dynamic-update-slice_fusion), channel_id=1, source_target_pairs={{0,4},{4,0},{8,12},{12,8},{1,5},{5,1},{9,13},{13,9},{2,6},{6,2},{1... | collective-permute-start | bytes 1032200 | tf_op jit(solution)/shard_map/ppermute | solution.py:12
  81.5 16.8 %collective-permute-start.12 = (bf16[192,896]{1,0:T(8,128)(2,1)S(1)}, bf16[192,896]{1,0:T(8,128)(2,1)S(1)}, u32[]{:S(2)}, u32[]{:S(2)}) collective-permute-start(bf16[192,896]{1,0:T(8,128)(2,1)S(1)} %constant_dynamic-update-slice_fusion.2), channel_id=1, source_target_pairs={{0,8},{4,12},{8,0},{12,4},{1,9},{5,13},{9,1},{13,5},{2,10},{6,14},... | collective-permute-start | bytes 1032200 | tf_op jit(solution)/shard_map/ppermute | solution.py:12
  83.5 19.7 %collective-permute-start.2 = (bf16[192,896]{1,0:T(8,128)(2,1)S(1)}, bf16[192,896]{1,0:T(8,128)(2,1)S(1)}, u32[]{:S(2)}, u32[]{:S(2)}) collective-permute-start(bf16[192,896]{1,0:T(8,128)(2,1)S(1)} %collective-permute-done.1), channel_id=1, source_target_pairs={{0,4},{4,0},{8,12},{12,8},{1,5},{5,1},{9,13},{13,9},{2,6},{6,2},{1... | collective-permute-start | bytes 1032200 | tf_op jit(solution)/shard_map/ppermute | solution.py:12
  86.8 34.9 %collective-permute-start.6 = (bf16[192,896]{1,0:T(8,128)(2,1)S(1)}, bf16[192,896]{1,0:T(8,128)(2,1)S(1)}, u32[]{:S(2)}, u32[]{:S(2)}) collective-permute-start(bf16[192,896]{1,0:T(8,128)(2,1)S(1)} %constant_dynamic-update-slice_fusion), channel_id=1, source_target_pairs={{0,3},{1,2},{2,1},{3,0},{4,7},{5,6},{6,5},{7,4},{8,11},{9,10},{10,... | collective-permute-start | bytes 1032200 | tf_op jit(solution)/shard_map/ppermute | solution.py:12
  89.9 44.9 %collective-permute-start.4 = (bf16[192,896]{1,0:T(8,128)(2,1)S(1)}, bf16[192,896]{1,0:T(8,128)(2,1)S(1)}, u32[]{:S(2)}, u32[]{:S(2)}) collective-permute-start(bf16[192,896]{1,0:T(8,128)(2,1)S(1)} %constant_dynamic-update-slice_fusion), channel_id=1, source_target_pairs={{0,1},{1,0},{2,3},{3,2},{4,5},{5,4},{6,7},{7,6},{8,9},{9,8},{10,11... | collective-permute-start | bytes 1032200 | tf_op jit(solution)/shard_map/ppermute | solution.py:12
  91.9 18.7 %collective-permute-start.14 = (bf16[192,896]{1,0:T(8,128)(2,1)S(1)}, bf16[192,896]{1,0:T(8,128)(2,1)S(1)}, u32[]{:S(2)}, u32[]{:S(2)}) collective-permute-start(bf16[192,896]{1,0:T(8,128)(2,1)S(1)} %constant_dynamic-update-slice_fusion.2), channel_id=1, source_target_pairs={{0,4},{4,0},{8,12},{12,8},{1,5},{5,1},{9,13},{13,9},{2,6},{6,2},{1... | collective-permute-start | bytes 1032200 | tf_op jit(solution)/shard_map/ppermute | solution.py:12
  98.4 19.6 %collective-permute-start.13 = (bf16[192,896]{1,0:T(8,128)(2,1)S(1)}, bf16[192,896]{1,0:T(8,128)(2,1)S(1)}, u32[]{:S(2)}, u32[]{:S(2)}) collective-permute-start(bf16[192,896]{1,0:T(8,128)(2,1)S(1)} %collective-permute-done.12), channel_id=1, source_target_pairs={{0,4},{4,0},{8,12},{12,8},{1,5},{5,1},{9,13},{13,9},{2,6},{6,2},{1... | collective-permute-start | bytes 1032200 | tf_op jit(solution)/shard_map/ppermute | solution.py:12
  103.4 21.0 %collective-permute-start.7 = (bf16[192,896]{1,0:T(8,128)(2,1)S(1)}, bf16[192,896]{1,0:T(8,128)(2,1)S(1)}, u32[]{:S(2)}, u32[]{:S(2)}) collective-permute-start(bf16[192,896]{1,0:T(8,128)(2,1)S(1)} %get-tuple-element.7), channel_id=1, source_target_pairs={{0,3},{1,2},{2,1},{3,0},{4,7},{5,6},{6,5},{7,4},{8,11},{9,10},{10,... | collective-permute-start | bytes 1032200 | tf_op jit(solution)/shard_map/ppermute | solution.py:12
  110.6 16.6 %collective-permute-start.8 = (bf16[192,896]{1,0:T(8,128)(2,1)S(1)}, bf16[192,896]{1,0:T(8,128)(2,1)S(1)}, u32[]{:S(2)}, u32[]{:S(2)}) collective-permute-start(bf16[192,896]{1,0:T(8,128)(2,1)S(1)} %constant_dynamic-update-slice_fusion), channel_id=1, source_target_pairs={{0,2},{1,3},{2,0},{3,1},{4,6},{5,7},{6,4},{7,5},{8,10},{9,11},{10,... | collective-permute-start | bytes 1032200 | tf_op jit(solution)/shard_map/ppermute | solution.py:12
  117.9 12.5 %collective-permute-start.9 = (bf16[192,896]{1,0:T(8,128)(2,1)S(1)}, bf16[192,896]{1,0:T(8,128)(2,1)S(1)}, u32[]{:S(2)}, u32[]{:S(2)}) collective-permute-start(bf16[192,896]{1,0:T(8,128)(2,1)S(1)} %get-tuple-element.6), channel_id=1, source_target_pairs={{0,2},{1,3},{2,0},{3,1},{4,6},{5,7},{6,4},{7,5},{8,10},{9,11},{10,... | collective-permute-start | bytes 1032200 | tf_op jit(solution)/shard_map/ppermute | solution.py:12
  121.7 20.7 %collective-permute-start.17 = (bf16[192,896]{1,0:T(8,128)(2,1)S(1)}, bf16[192,896]{1,0:T(8,128)(2,1)S(1)}, u32[]{:S(2)}, u32[]{:S(2)}) collective-permute-start(bf16[192,896]{1,0:T(8,128)(2,1)S(1)} %constant_dynamic-update-slice_fusion.2), channel_id=1, source_target_pairs={{0,3},{1,2},{2,1},{3,0},{4,7},{5,6},{6,5},{7,4},{8,11},{9,10},{10,... | collective-permute-start | bytes 1032200 | tf_op jit(solution)/shard_map/ppermute | solution.py:12
  124.4 12.5 %collective-permute-start.5 = (bf16[192,896]{1,0:T(8,128)(2,1)S(1)}, bf16[192,896]{1,0:T(8,128)(2,1)S(1)}, u32[]{:S(2)}, u32[]{:S(2)}) collective-permute-start(bf16[192,896]{1,0:T(8,128)(2,1)S(1)} %get-tuple-element.5), channel_id=1, source_target_pairs={{0,1},{1,0},{2,3},{3,2},{4,5},{5,4},{6,7},{7,6},{8,9},{9,8},{10,11... | collective-permute-start | bytes 1032200 | tf_op jit(solution)/shard_map/ppermute | solution.py:12
  127.2 32.6 %collective-permute-start.15 = (bf16[192,896]{1,0:T(8,128)(2,1)S(1)}, bf16[192,896]{1,0:T(8,128)(2,1)S(1)}, u32[]{:S(2)}, u32[]{:S(2)}) collective-permute-start(bf16[192,896]{1,0:T(8,128)(2,1)S(1)} %constant_dynamic-update-slice_fusion.2), channel_id=1, source_target_pairs={{0,1},{1,0},{2,3},{3,2},{4,5},{5,4},{6,7},{7,6},{8,9},{9,8},{10,11... | collective-permute-start | bytes 1032200 | tf_op jit(solution)/shard_map/ppermute | solution.py:12
  130.4 16.3 %collective-permute-start.18 = (bf16[192,896]{1,0:T(8,128)(2,1)S(1)}, bf16[192,896]{1,0:T(8,128)(2,1)S(1)}, u32[]{:S(2)}, u32[]{:S(2)}) collective-permute-start(bf16[192,896]{1,0:T(8,128)(2,1)S(1)} %get-tuple-element.10), channel_id=1, source_target_pairs={{0,3},{1,2},{2,1},{3,0},{4,7},{5,6},{6,5},{7,4},{8,11},{9,10},{10,... | collective-permute-start | bytes 1032200 | tf_op jit(solution)/shard_map/ppermute | solution.py:12
  134.9 16.9 %collective-permute-start.19 = (bf16[192,896]{1,0:T(8,128)(2,1)S(1)}, bf16[192,896]{1,0:T(8,128)(2,1)S(1)}, u32[]{:S(2)}, u32[]{:S(2)}) collective-permute-start(bf16[192,896]{1,0:T(8,128)(2,1)S(1)} %constant_dynamic-update-slice_fusion.2), channel_id=1, source_target_pairs={{0,2},{1,3},{2,0},{3,1},{4,6},{5,7},{6,4},{7,5},{8,10},{9,11},{10,... | collective-permute-start | bytes 1032200 | tf_op jit(solution)/shard_map/ppermute | solution.py:12
  136.9 22.2 %collective-permute-start.20 = (bf16[192,896]{1,0:T(8,128)(2,1)S(1)}, bf16[192,896]{1,0:T(8,128)(2,1)S(1)}, u32[]{:S(2)}, u32[]{:S(2)}) collective-permute-start(bf16[192,896]{1,0:T(8,128)(2,1)S(1)} %get-tuple-element.9), channel_id=1, source_target_pairs={{0,2},{1,3},{2,0},{3,1},{4,6},{5,7},{6,4},{7,5},{8,10},{9,11},{10,... | collective-permute-start | bytes 1032200 | tf_op jit(solution)/shard_map/ppermute | solution.py:12
  142.4 23.5 %collective-permute-start.16 = (bf16[192,896]{1,0:T(8,128)(2,1)S(1)}, bf16[192,896]{1,0:T(8,128)(2,1)S(1)}, u32[]{:S(2)}, u32[]{:S(2)}) collective-permute-start(bf16[192,896]{1,0:T(8,128)(2,1)S(1)} %get-tuple-element.8), channel_id=1, source_target_pairs={{0,1},{1,0},{2,3},{3,2},{4,5},{5,4},{6,7},{7,6},{8,9},{9,8},{10,11... | collective-permute-start | bytes 1032200 | tf_op jit(solution)/shard_map/ppermute | solution.py:12
where the time goes:
time: 171 us; the launch traced here: 170 us
  starting transfers between devices  74.8 us (44%)
  waiting for transfers between devices  61.8 us (36%)
  blocking collectives  20.4 us (12%)
  matrix products  9.11 us (5%)
  other arithmetic  1.83 us (1%)
    ppermute x18, starting transfers between devices, swap(): return lax.ppermute(rows, axis, [(i, i ^ mask) for i in range(SIDE)])  48.4 us
    ppermute x18, waiting for transfers between devices, swap(): return lax.ppermute(rows, axis, [(i, i ^ mask) for i in range(SIDE)])  33.8 us
    ppermute x3, waiting for transfers between devices, reach(): lax.ppermute(rows, 'expert', [(e, e ^ d * CHIPS) for e in range(SEGMENTS...  28.1 us
    ppermute x3, starting transfers between devices, reach(): lax.ppermute(rows, 'expert', [(e, e ^ d * CHIPS) for e in range(SEGMENTS...  26.3 us
    all_to_all x1, blocking collectives, per_device(): lax.all_to_all(outgoing.reshape(CHIPS, -1, width), 'expert', 0, 0, tiled=...  20.4 us
    dot_general x8, matrix products, per_device(): lax.dot_general(left, right, (((0,), (0,)), ((), ())), preferred_element_...  7.85 us
  transfers between devices with their start and end apart: 21, of which 10 were waited for; matrix products, arithmetic and copies ran while one was open for 3% of the time, Pallas kernels for 0%

commit v1 on v0

--- a/solution.py
+++ b/solution.py
@@ -31,15 +31,13 @@
     return rows.reshape(groups, panels * slot_count, tokens.shape[1]), totals
 
 
-def moment_parts(rows):
-    lefts = [rows] + [swap(rows, "col", m) for m in (1, 3, 2)]
-    far = swap(rows, "row", 2)
-    near = swap(rows, "row", 1)
-    features = [rows, near, far, swap(far, "row", 1)]
-    here = lax.axis_index("row") ^ lax.axis_index("col")
-    picked = [pick(features, here ^ m) for m in (0, 1, 3, 2)]
-    rights = [picked[0]] + [swap(q, "col", m) for q, m in zip(picked[1:], (1, 3, 2))]
-    return list(zip(lefts, rights))
+def direct_parts(rows):
+    lefts = [rows] + [swap(rows, "col", m) for m in (1, 2, 3)]
+    out = []
+    for k in range(SIDE):
+        pairs = [(l * SIDE + c, (c ^ l ^ k) * SIDE + l) for l in range(SIDE) for c in range(SIDE)]
+        out.append((pick(lefts, lax.axis_index("row") ^ k), lax.ppermute(rows, ("row", "col"), pairs)))
+    return out
 
 
 def pick(choices, index):
@@ -64,7 +62,7 @@
   tile = None
   for group in ((0, 1), (3, 2)):
       part = jnp.concatenate([pieces[d] for d in group])
-      for left, right in moment_parts(part):
+      for left, right in (direct_parts)(part):
           term = lax.dot_general(left, right, (((0,), (0,)), ((), ())), preferred_element_type=jnp.float32)
           tile = term if tile is None else tile + term
   return (tile / total)[None]

time: 171 us -> 167 us (0.977)
  the two profiles are of different devices: /device:TPU:1 before, /device:TPU:401 now
where the time goes in v1:
time: 167 us; the launch traced here: 166 us
  starting transfers between devices  83.4 us (50%)
  waiting for transfers between devices  54.5 us (33%)
  blocking collectives  16 us (10%)
  matrix products  9.22 us (6%)
    ppermute x8, starting transfers between devices, direct_parts(): lax.ppermute(rows, ('row', 'col'), pairs)  45.4 us
    ppermute x8, waiting for transfers between devices, direct_parts(): lax.ppermute(rows, ('row', 'col'), pairs)  37.2 us
    ppermute x6, starting transfers between devices, swap(): return lax.ppermute(rows, axis, [(i, i ^ mask) for i in range(SIDE)])  21.8 us
    ppermute x3, waiting for transfers between devices, reach(): lax.ppermute(rows, 'expert', [(e, e ^ d * CHIPS) for e in range(SEGMENTS...  17.3 us
    ppermute x3, starting transfers between devices, reach(): lax.ppermute(rows, 'expert', [(e, e ^ d * CHIPS) for e in range(SEGMENTS...  16.2 us
    all_to_all x1, blocking collectives, per_device(): lax.all_to_all(outgoing.reshape(CHIPS, -1, width), 'expert', 0, 0, tiled=...  16 us
    dot_general x8, matrix products, per_device(): lax.dot_general(left, right, (((0,), (0,)), ((), ())), preferred_element_...  7.96 us
  transfers between devices with their start and end apart: 17, of which 6 were waited for; matrix products, arithmetic and copies ran while one was open for 3% of the time, Pallas kernels for 0%

profile of v1, /device:TPU:401, one launch (start us, length us, event | category | flops | bytes accessed | tf_op | source)
XLA Modules:
  0.0 166.2 jit_solution(17926728246242708871)
XLA Ops:
  0.0 0.8 fusion.63
  0.9 0.8 convolution_convert_fusion.1
  1.7 0.1 copy.5
  1.8 0.1 eq.88
  1.9 0.0 copy-start.1
  2.0 0.4 convolution_convert_fusion
  2.4 16.0 %all_to_all.5 = bf16[8,48,896]{2,1,0:T(8,128)(2,1)S(1)} all-to-all(bf16[8,48,896]{2,1,0:T(8,128)(2,1)S(1)} %bitcast.19), channel_id=1, replica_groups={{0,16,32,48,64,80,96,112},{128,144,160,176,192,208,224,240},{256,272,28..., dimensions={0} | all-to-all | bytes 1376256 | tf_op jit(solution)/shard_map/all_to_all | solution.py:58
  18.4 0.1 fusion.67
  18.5 5.2 %collective-permute-start = (bf16[96,896]{1,0:T(8,128)(2,1)S(1)}, bf16[96,896]{1,0:T(8,128)(2,1)S(1)}, u32[]{:S(2)}, u32[]{:S(2)}) collective-permute-start(bf16[96,896]{1,0:T(8,128)(2,1)S(1)} %reshape.48), channel_id=1, source_target_pairs={{0,128},{16,144},{32,160},{48,176},{64,192},{80,208},{96,224},{112... | collective-permute-start | bytes 516104 | tf_op jit(solution)/shard_map/ppermute | solution.py:51
  23.9 1.9 %collective-permute-start.8 = (bf16[96,896]{1,0:T(8,128)(2,1)S(1)}, bf16[96,896]{1,0:T(8,128)(2,1)S(1)}, u32[]{:S(2)}, u32[]{:S(2)}) collective-permute-start(bf16[96,896]{1,0:T(8,128)(2,1)S(1)} %reshape.49), channel_id=1, source_target_pairs={{0,384},{16,400},{32,416},{48,432},{64,448},{80,464},{96,480},{112... | collective-permute-start | bytes 516104 | tf_op jit(solution)/shard_map/ppermute | solution.py:51
  25.9 9.1 %collective-permute-start.9 = (bf16[96,896]{1,0:T(8,128)(2,1)S(1)}, bf16[96,896]{1,0:T(8,128)(2,1)S(1)}, u32[]{:S(2)}, u32[]{:S(2)}) collective-permute-start(bf16[96,896]{1,0:T(8,128)(2,1)S(1)} %reshape.50), channel_id=1, source_target_pairs={{0,256},{16,272},{32,288},{48,304},{64,320},{80,336},{96,352},{112... | collective-permute-start | bytes 516104 | tf_op jit(solution)/shard_map/ppermute | solution.py:51
  35.0 2.0 %collective-permute-done = bf16[96,896]{1,0:T(8,128)(2,1)S(1)} collective-permute-done((bf16[96,896]{1,0:T(8,128)(2,1)S(1)}, bf16[96,896]{1,0:T(8,128)(2,1)S(1)}, u32[]{:S(2)}, u32[]{:S(2)}) %collective-permute-start) | collective-permute-done | bytes 172064 | tf_op jit(solution)/shard_map/ppermute | solution.py:51
  37.0 2.1 %collective-permute-start.1 = (bf16[192,896]{1,0:T(8,128)(2,1)S(1)}, bf16[192,896]{1,0:T(8,128)(2,1)S(1)}, u32[]{:S(2)}, u32[]{:S(2)}) collective-permute-start(bf16[192,896]{1,0:T(8,128)(2,1)S(1)} %constant_dynamic-update-slice_fusion), channel_id=1, source_target_pairs={{0,3},{1,2},{2,1},{3,0},{4,7},{5,6},{6,5},{7,4},{8,11},{9,10},{10,... | collective-permute-start | bytes 1032200 | tf_op jit(solution)/shard_map/ppermute | solution.py:12
  39.1 4.5 %collective-permute-start.2 = (bf16[192,896]{1,0:T(8,128)(2,1)S(1)}, bf16[192,896]{1,0:T(8,128)(2,1)S(1)}, u32[]{:S(2)}, u32[]{:S(2)}) collective-permute-start(bf16[192,896]{1,0:T(8,128)(2,1)S(1)} %constant_dynamic-update-slice_fusion), channel_id=1, source_target_pairs={{0,2},{1,3},{2,0},{3,1},{4,6},{5,7},{6,4},{7,5},{8,10},{9,11},{10,... | collective-permute-start | bytes 1032200 | tf_op jit(solution)/shard_map/ppermute | solution.py:12
  43.7 2.4 %collective-permute-start.3 = (bf16[192,896]{1,0:T(8,128)(2,1)S(1)}, bf16[192,896]{1,0:T(8,128)(2,1)S(1)}, u32[]{:S(2)}, u32[]{:S(2)}) collective-permute-start(bf16[192,896]{1,0:T(8,128)(2,1)S(1)} %constant_dynamic-update-slice_fusion), channel_id=1, source_target_pairs={{0,1},{1,0},{2,3},{3,2},{4,5},{5,4},{6,7},{7,6},{8,9},{9,8},{10,11... | collective-permute-start | bytes 1032200 | tf_op jit(solution)/shard_map/ppermute | solution.py:12
  46.0 15.3 %collective-permute-done.8 = bf16[96,896]{1,0:T(8,128)(2,1)S(1)} collective-permute-done((bf16[96,896]{1,0:T(8,128)(2,1)S(1)}, bf16[96,896]{1,0:T(8,128)(2,1)S(1)}, u32[]{:S(2)}, u32[]{:S(2)}) %collective-permute-start.8) | collective-permute-done | bytes 172064 | tf_op jit(solution)/shard_map/ppermute | solution.py:51
  61.3 1.9 %collective-permute-start.5 = (bf16[192,896]{1,0:T(8,128)(2,1)S(1)}, bf16[192,896]{1,0:T(8,128)(2,1)S(1)}, u32[]{:S(2)}, u32[]{:S(2)}) collective-permute-start(bf16[192,896]{1,0:T(8,128)(2,1)S(1)} %constant_dynamic-update-slice_fusion), channel_id=1, source_target_pairs={{0,4},{1,0},{2,12},{3,8},{4,1},{5,5},{6,9},{7,13},{8,14},{9,10},{1... | collective-permute-start | bytes 1032200 | tf_op jit(solution)/shard_map/ppermute | solution.py:39
  63.2 0.6 select_reduce_fusion
  64.5 1.9 %collective-permute-start.4 = (bf16[192,896]{1,0:T(8,128)(2,1)S(1)}, bf16[192,896]{1,0:T(8,128)(2,1)S(1)}, u32[]{:S(2)}, u32[]{:S(2)}) collective-permute-start(bf16[192,896]{1,0:T(8,128)(2,1)S(1)} %constant_dynamic-update-slice_fusion), channel_id=1, source_target_pairs={{0,0},{1,4},{2,8},{3,12},{4,5},{5,1},{6,13},{7,9},{8,10},{9,14},{1... | collective-permute-start | bytes 1032200 | tf_op jit(solution)/shard_map/ppermute | solution.py:39
  66.5 0.0 collective-permute-done.1
  66.5 1.9 %collective-permute-start.6 = (bf16[192,896]{1,0:T(8,128)(2,1)S(1)}, bf16[192,896]{1,0:T(8,128)(2,1)S(1)}, u32[]{:S(2)}, u32[]{:S(2)}) collective-permute-start(bf16[192,896]{1,0:T(8,128)(2,1)S(1)} %constant_dynamic-update-slice_fusion), channel_id=1, source_target_pairs={{0,8},{1,12},{2,0},{3,4},{4,13},{5,9},{6,5},{7,1},{8,2},{9,6},{10,... | collective-permute-start | bytes 1032200 | tf_op jit(solution)/shard_map/ppermute | solution.py:39
  68.4 0.0 collective-permute-done.2
  68.5 4.4 %collective-permute-start.10 = (bf16[192,896]{1,0:T(8,128)(2,1)S(1)}, bf16[192,896]{1,0:T(8,128)(2,1)S(1)}, u32[]{:S(2)}, u32[]{:S(2)}) collective-permute-start(bf16[192,896]{1,0:T(8,128)(2,1)S(1)} %constant_dynamic-update-slice_fusion.2), channel_id=1, source_target_pairs={{0,3},{1,2},{2,1},{3,0},{4,7},{5,6},{6,5},{7,4},{8,11},{9,10},{10,... | collective-permute-start | bytes 1032200 | tf_op jit(solution)/shard_map/ppermute | solution.py:12
  72.9 0.0 collective-permute-done.3
  72.9 6.5 %collective-permute-start.11 = (bf16[192,896]{1,0:T(8,128)(2,1)S(1)}, bf16[192,896]{1,0:T(8,128)(2,1)S(1)}, u32[]{:S(2)}, u32[]{:S(2)}) collective-permute-start(bf16[192,896]{1,0:T(8,128)(2,1)S(1)} %constant_dynamic-update-slice_fusion.2), channel_id=1, source_target_pairs={{0,2},{1,3},{2,0},{3,1},{4,6},{5,7},{6,4},{7,5},{8,10},{9,11},{10,... | collective-permute-start | bytes 1032200 | tf_op jit(solution)/shard_map/ppermute | solution.py:12
  79.4 6.2 %collective-permute-done.5 = bf16[192,896]{1,0:T(8,128)(2,1)S(1)} collective-permute-done((bf16[192,896]{1,0:T(8,128)(2,1)S(1)}, bf16[192,896]{1,0:T(8,128)(2,1)S(1)}, u32[]{:S(2)}, u32[]{:S(2)}) %collective-permute-start.5) | collective-permute-done | bytes 344096 | tf_op jit(solution)/shard_map/ppermute | solution.py:39
  85.6 1.9 %collective-permute-start.12 = (bf16[192,896]{1,0:T(8,128)(2,1)S(1)}, bf16[192,896]{1,0:T(8,128)(2,1)S(1)}, u32[]{:S(2)}, u32[]{:S(2)}) collective-permute-start(bf16[192,896]{1,0:T(8,128)(2,1)S(1)} %constant_dynamic-update-slice_fusion.2), channel_id=1, source_target_pairs={{0,1},{1,0},{2,3},{3,2},{4,5},{5,4},{6,7},{7,6},{8,9},{9,8},{10,11... | collective-permute-start | bytes 1032200 | tf_op jit(solution)/shard_map/ppermute | solution.py:12
  87.6 0.7 fusion.26
  88.2 1.1 collective-permute-done.4
  89.4 4.1 %collective-permute-start.13 = (bf16[192,896]{1,0:T(8,128)(2,1)S(1)}, bf16[192,896]{1,0:T(8,128)(2,1)S(1)}, u32[]{:S(2)}, u32[]{:S(2)}) collective-permute-start(bf16[192,896]{1,0:T(8,128)(2,1)S(1)} %constant_dynamic-update-slice_fusion.2), channel_id=1, source_target_pairs={{0,0},{1,4},{2,8},{3,12},{4,5},{5,1},{6,13},{7,9},{8,10},{9,14},{1... | collective-permute-start | bytes 1032200 | tf_op jit(solution)/shard_map/ppermute | solution.py:39
  93.4 0.7 fusion.30
  94.1 0.0 collective-permute-done.10
  94.1 8.5 %collective-permute-start.7 = (bf16[192,896]{1,0:T(8,128)(2,1)S(1)}, bf16[192,896]{1,0:T(8,128)(2,1)S(1)}, u32[]{:S(2)}, u32[]{:S(2)}) collective-permute-start(bf16[192,896]{1,0:T(8,128)(2,1)S(1)} %constant_dynamic-update-slice_fusion), channel_id=1, source_target_pairs={{0,12},{1,8},{2,4},{3,0},{4,9},{5,13},{6,1},{7,5},{8,6},{9,2},{10,... | collective-permute-start | bytes 1032200 | tf_op jit(solution)/shard_map/ppermute | solution.py:39
  102.6 0.0 collective-permute-done.11
  102.6 7.4 %collective-permute-start.14 = (bf16[192,896]{1,0:T(8,128)(2,1)S(1)}, bf16[192,896]{1,0:T(8,128)(2,1)S(1)}, u32[]{:S(2)}, u32[]{:S(2)}) collective-permute-start(bf16[192,896]{1,0:T(8,128)(2,1)S(1)} %constant_dynamic-update-slice_fusion.2), channel_id=1, source_target_pairs={{0,4},{1,0},{2,12},{3,8},{4,1},{5,5},{6,9},{7,13},{8,14},{9,10},{1... | collective-permute-start | bytes 1032200 | tf_op jit(solution)/shard_map/ppermute | solution.py:39
  110.0 0.0 collective-permute-done.12
  110.0 1.9 %collective-permute-start.15 = (bf16[192,896]{1,0:T(8,128)(2,1)S(1)}, bf16[192,896]{1,0:T(8,128)(2,1)S(1)}, u32[]{:S(2)}, u32[]{:S(2)}) collective-permute-start(bf16[192,896]{1,0:T(8,128)(2,1)S(1)} %constant_dynamic-update-slice_fusion.2), channel_id=1, source_target_pairs={{0,8},{1,12},{2,0},{3,4},{4,13},{5,9},{6,5},{7,1},{8,2},{9,6},{10,... | collective-permute-start | bytes 1032200 | tf_op jit(solution)/shard_map/ppermute | solution.py:39
  111.9 0.0 collective-permute-done.13
  111.9 17.8 %collective-permute-start.16 = (bf16[192,896]{1,0:T(8,128)(2,1)S(1)}, bf16[192,896]{1,0:T(8,128)(2,1)S(1)}, u32[]{:S(2)}, u32[]{:S(2)}) collective-permute-start(bf16[192,896]{1,0:T(8,128)(2,1)S(1)} %constant_dynamic-update-slice_fusion.2), channel_id=1, source_target_pairs={{0,12},{1,8},{2,4},{3,0},{4,9},{5,13},{6,1},{7,5},{8,6},{9,2},{10,... | collective-permute-start | bytes 1032200 | tf_op jit(solution)/shard_map/ppermute | solution.py:39
  129.7 0.7 fusion.14
  130.4 0.0 collective-permute-done.14
  130.4 0.7 fusion.10
  131.1 0.7 fusion.22
  131.8 18.0 %collective-permute-done.15 = bf16[192,896]{1,0:T(8,128)(2,1)S(1)} collective-permute-done((bf16[192,896]{1,0:T(8,128)(2,1)S(1)}, bf16[192,896]{1,0:T(8,128)(2,1)S(1)}, u32[]{:S(2)}, u32[]{:S(2)}) %collective-permute-start.15) | collective-permute-done | bytes 344096 | tf_op jit(solution)/shard_map/ppermute | solution.py:39
  149.8 0.7 fusion.6
  150.5 0.7 fusion.18
  151.1 11.9 %collective-permute-done.16 = bf16[192,896]{1,0:T(8,128)(2,1)S(1)} collective-permute-done((bf16[192,896]{1,0:T(8,128)(2,1)S(1)}, bf16[192,896]{1,0:T(8,128)(2,1)S(1)}, u32[]{:S(2)}, u32[]{:S(2)}) %collective-permute-start.16) | collective-permute-done | bytes 344096 | tf_op jit(solution)/shard_map/ppermute | solution.py:39
  163.0 3.2 %divide_bitcast_fusion = f32[1,896,896]{2,1,0:T(8,128)} fusion(f32[896,896]{1,0:T(8,128)S(1)} %fusion.6, f32[896,896]{1,0:T(8,128)S(1)} %fusion.10, f32[896,896]{1,0:T(8,128)S(1)} %fusion.14, f32[896,896]{1,0:T(8,128)S(1)} %fusion.18, f32[896,896]{1,0:T(8,128)S(1)} %fusion.22, f32[896,896]{1,0:T(8,128)S(1)} %fusion.30, f32[896,896]{1,0:T(8,128)S(1)} %fusion.26, ...), kind=kOutput, calls=%fused_computation | convolution fusion | flops 315219968 | bytes 27410440 | tf_op jit(solution)/shard_map/dot_general | solution.py:66
  (20 shorter events, 0.3 us)
Async XLA Ops:
  0.0 1.9 %copy-start = (bf16[256,896]{1,0:T(8,128)(2,1)S(1)}, bf16[256,896]{1,0:T(8,128)(2,1)}, u32[]{:S(2)}) copy-start(bf16[256,896]{1,0:T(8,128)(2,1)} %param.4) | copy-start | bytes 1376260
  0.0 23.7 %copy-start.2 = (s32[32]{0:T(128)S(1)}, s32[32]{0:T(128)}, u32[]{:S(2)}) copy-start(s32[32]{0:T(128)} %param.7) | copy-start | bytes 388
  1.9 61.3 %copy-start.1 = (s32[6,32]{1,0:T(8,128)S(1)}, s32[6,32]{1,0:T(8,128)}, u32[]{:S(2)}) copy-start(s32[6,32]{1,0:T(8,128)} %param.6) | copy-start | bytes 2308
  18.5 18.5 %collective-permute-start = (bf16[96,896]{1,0:T(8,128)(2,1)S(1)}, bf16[96,896]{1,0:T(8,128)(2,1)S(1)}, u32[]{:S(2)}, u32[]{:S(2)}) collective-permute-start(bf16[96,896]{1,0:T(8,128)(2,1)S(1)} %reshape.48), channel_id=1, source_target_pairs={{0,128},{16,144},{32,160},{48,176},{64,192},{80,208},{96,224},{112... | collective-permute-start | bytes 516104 | tf_op jit(solution)/shard_map/ppermute | solution.py:51
  23.9 37.4 %collective-permute-start.8 = (bf16[96,896]{1,0:T(8,128)(2,1)S(1)}, bf16[96,896]{1,0:T(8,128)(2,1)S(1)}, u32[]{:S(2)}, u32[]{:S(2)}) collective-permute-start(bf16[96,896]{1,0:T(8,128)(2,1)S(1)} %reshape.49), channel_id=1, source_target_pairs={{0,384},{16,400},{32,416},{48,432},{64,448},{80,464},{96,480},{112... | collective-permute-start | bytes 516104 | tf_op jit(solution)/shard_map/ppermute | solution.py:51
  25.9 38.7 %collective-permute-start.9 = (bf16[96,896]{1,0:T(8,128)(2,1)S(1)}, bf16[96,896]{1,0:T(8,128)(2,1)S(1)}, u32[]{:S(2)}, u32[]{:S(2)}) collective-permute-start(bf16[96,896]{1,0:T(8,128)(2,1)S(1)} %reshape.50), channel_id=1, source_target_pairs={{0,256},{16,272},{32,288},{48,304},{64,320},{80,336},{96,352},{112... | collective-permute-start | bytes 516104 | tf_op jit(solution)/shard_map/ppermute | solution.py:51
  37.0 29.5 %collective-permute-start.1 = (bf16[192,896]{1,0:T(8,128)(2,1)S(1)}, bf16[192,896]{1,0:T(8,128)(2,1)S(1)}, u32[]{:S(2)}, u32[]{:S(2)}) collective-permute-start(bf16[192,896]{1,0:T(8,128)(2,1)S(1)} %constant_dynamic-update-slice_fusion), channel_id=1, source_target_pairs={{0,3},{1,2},{2,1},{3,0},{4,7},{5,6},{6,5},{7,4},{8,11},{9,10},{10,... | collective-permute-start | bytes 1032200 | tf_op jit(solution)/shard_map/ppermute | solution.py:12
  39.1 29.3 %collective-permute-start.2 = (bf16[192,896]{1,0:T(8,128)(2,1)S(1)}, bf16[192,896]{1,0:T(8,128)(2,1)S(1)}, u32[]{:S(2)}, u32[]{:S(2)}) collective-permute-start(bf16[192,896]{1,0:T(8,128)(2,1)S(1)} %constant_dynamic-update-slice_fusion), channel_id=1, source_target_pairs={{0,2},{1,3},{2,0},{3,1},{4,6},{5,7},{6,4},{7,5},{8,10},{9,11},{10,... | collective-permute-start | bytes 1032200 | tf_op jit(solution)/shard_map/ppermute | solution.py:12
  43.7 29.2 %collective-permute-start.3 = (bf16[192,896]{1,0:T(8,128)(2,1)S(1)}, bf16[192,896]{1,0:T(8,128)(2,1)S(1)}, u32[]{:S(2)}, u32[]{:S(2)}) collective-permute-start(bf16[192,896]{1,0:T(8,128)(2,1)S(1)} %constant_dynamic-update-slice_fusion), channel_id=1, source_target_pairs={{0,1},{1,0},{2,3},{3,2},{4,5},{5,4},{6,7},{7,6},{8,9},{9,8},{10,11... | collective-permute-start | bytes 1032200 | tf_op jit(solution)/shard_map/ppermute | solution.py:12
  61.3 24.3 %collective-permute-start.5 = (bf16[192,896]{1,0:T(8,128)(2,1)S(1)}, bf16[192,896]{1,0:T(8,128)(2,1)S(1)}, u32[]{:S(2)}, u32[]{:S(2)}) collective-permute-start(bf16[192,896]{1,0:T(8,128)(2,1)S(1)} %constant_dynamic-update-slice_fusion), channel_id=1, source_target_pairs={{0,4},{1,0},{2,12},{3,8},{4,1},{5,5},{6,9},{7,13},{8,14},{9,10},{1... | collective-permute-start | bytes 1032200 | tf_op jit(solution)/shard_map/ppermute | solution.py:39
  64.5 24.8 %collective-permute-start.4 = (bf16[192,896]{1,0:T(8,128)(2,1)S(1)}, bf16[192,896]{1,0:T(8,128)(2,1)S(1)}, u32[]{:S(2)}, u32[]{:S(2)}) collective-permute-start(bf16[192,896]{1,0:T(8,128)(2,1)S(1)} %constant_dynamic-update-slice_fusion), channel_id=1, source_target_pairs={{0,0},{1,4},{2,8},{3,12},{4,5},{5,1},{6,13},{7,9},{8,10},{9,14},{1... | collective-permute-start | bytes 1032200 | tf_op jit(solution)/shard_map/ppermute | solution.py:39
  66.5 64.6 %collective-permute-start.6 = (bf16[192,896]{1,0:T(8,128)(2,1)S(1)}, bf16[192,896]{1,0:T(8,128)(2,1)S(1)}, u32[]{:S(2)}, u32[]{:S(2)}) collective-permute-start(bf16[192,896]{1,0:T(8,128)(2,1)S(1)} %constant_dynamic-update-slice_fusion), channel_id=1, source_target_pairs={{0,8},{1,12},{2,0},{3,4},{4,13},{5,9},{6,5},{7,1},{8,2},{9,6},{10,... | collective-permute-start | bytes 1032200 | tf_op jit(solution)/shard_map/ppermute | solution.py:39
  68.5 25.7 %collective-permute-start.10 = (bf16[192,896]{1,0:T(8,128)(2,1)S(1)}, bf16[192,896]{1,0:T(8,128)(2,1)S(1)}, u32[]{:S(2)}, u32[]{:S(2)}) collective-permute-start(bf16[192,896]{1,0:T(8,128)(2,1)S(1)} %constant_dynamic-update-slice_fusion.2), channel_id=1, source_target_pairs={{0,3},{1,2},{2,1},{3,0},{4,7},{5,6},{6,5},{7,4},{8,11},{9,10},{10,... | collective-permute-start | bytes 1032200 | tf_op jit(solution)/shard_map/ppermute | solution.py:12
  72.9 29.7 %collective-permute-start.11 = (bf16[192,896]{1,0:T(8,128)(2,1)S(1)}, bf16[192,896]{1,0:T(8,128)(2,1)S(1)}, u32[]{:S(2)}, u32[]{:S(2)}) collective-permute-start(bf16[192,896]{1,0:T(8,128)(2,1)S(1)} %constant_dynamic-update-slice_fusion.2), channel_id=1, source_target_pairs={{0,2},{1,3},{2,0},{3,1},{4,6},{5,7},{6,4},{7,5},{8,10},{9,11},{10,... | collective-permute-start | bytes 1032200 | tf_op jit(solution)/shard_map/ppermute | solution.py:12
  85.6 24.4 %collective-permute-start.12 = (bf16[192,896]{1,0:T(8,128)(2,1)S(1)}, bf16[192,896]{1,0:T(8,128)(2,1)S(1)}, u32[]{:S(2)}, u32[]{:S(2)}) collective-permute-start(bf16[192,896]{1,0:T(8,128)(2,1)S(1)} %constant_dynamic-update-slice_fusion.2), channel_id=1, source_target_pairs={{0,1},{1,0},{2,3},{3,2},{4,5},{5,4},{6,7},{7,6},{8,9},{9,8},{10,11... | collective-permute-start | bytes 1032200 | tf_op jit(solution)/shard_map/ppermute | solution.py:12
  89.4 22.6 %collective-permute-start.13 = (bf16[192,896]{1,0:T(8,128)(2,1)S(1)}, bf16[192,896]{1,0:T(8,128)(2,1)S(1)}, u32[]{:S(2)}, u32[]{:S(2)}) collective-permute-start(bf16[192,896]{1,0:T(8,128)(2,1)S(1)} %constant_dynamic-update-slice_fusion.2), channel_id=1, source_target_pairs={{0,0},{1,4},{2,8},{3,12},{4,5},{5,1},{6,13},{7,9},{8,10},{9,14},{1... | collective-permute-start | bytes 1032200 | tf_op jit(solution)/shard_map/ppermute | solution.py:39
  94.1 56.3 %collective-permute-start.7 = (bf16[192,896]{1,0:T(8,128)(2,1)S(1)}, bf16[192,896]{1,0:T(8,128)(2,1)S(1)}, u32[]{:S(2)}, u32[]{:S(2)}) collective-permute-start(bf16[192,896]{1,0:T(8,128)(2,1)S(1)} %constant_dynamic-update-slice_fusion), channel_id=1, source_target_pairs={{0,12},{1,8},{2,4},{3,0},{4,9},{5,13},{6,1},{7,5},{8,6},{9,2},{10,... | collective-permute-start | bytes 1032200 | tf_op jit(solution)/shard_map/ppermute | solution.py:39
  102.6 27.8 %collective-permute-start.14 = (bf16[192,896]{1,0:T(8,128)(2,1)S(1)}, bf16[192,896]{1,0:T(8,128)(2,1)S(1)}, u32[]{:S(2)}, u32[]{:S(2)}) collective-permute-start(bf16[192,896]{1,0:T(8,128)(2,1)S(1)} %constant_dynamic-update-slice_fusion.2), channel_id=1, source_target_pairs={{0,4},{1,0},{2,12},{3,8},{4,1},{5,5},{6,9},{7,13},{8,14},{9,10},{1... | collective-permute-start | bytes 1032200 | tf_op jit(solution)/shard_map/ppermute | solution.py:39
  110.0 39.8 %collective-permute-start.15 = (bf16[192,896]{1,0:T(8,128)(2,1)S(1)}, bf16[192,896]{1,0:T(8,128)(2,1)S(1)}, u32[]{:S(2)}, u32[]{:S(2)}) collective-permute-start(bf16[192,896]{1,0:T(8,128)(2,1)S(1)} %constant_dynamic-update-slice_fusion.2), channel_id=1, source_target_pairs={{0,8},{1,12},{2,0},{3,4},{4,13},{5,9},{6,5},{7,1},{8,2},{9,6},{10,... | collective-permute-start | bytes 1032200 | tf_op jit(solution)/shard_map/ppermute | solution.py:39
  111.9 51.1 %collective-permute-start.16 = (bf16[192,896]{1,0:T(8,128)(2,1)S(1)}, bf16[192,896]{1,0:T(8,128)(2,1)S(1)}, u32[]{:S(2)}, u32[]{:S(2)}) collective-permute-start(bf16[192,896]{1,0:T(8,128)(2,1)S(1)} %constant_dynamic-update-slice_fusion.2), channel_id=1, source_target_pairs={{0,12},{1,8},{2,4},{3,0},{4,9},{5,13},{6,1},{7,5},{8,6},{9,2},{10,... | collective-permute-start | bytes 1032200 | tf_op jit(solution)/shard_map/ppermute | solution.py:39

commit v2 on v1

--- a/solution.py
+++ b/solution.py
@@ -35,8 +35,10 @@
     lefts = [rows] + [swap(rows, "col", m) for m in (1, 2, 3)]
     out = []
     for k in range(SIDE):
-        pairs = [(l * SIDE + c, (c ^ l ^ k) * SIDE + l) for l in range(SIDE) for c in range(SIDE)]
-        out.append((pick(lefts, lax.axis_index("row") ^ k), lax.ppermute(rows, ("row", "col"), pairs)))
+        pairs = [(l * SIDE + c, (c ^ l ^ k) * SIDE + l) for l in range(SIDE) for c in range(SIDE) if c != k]
+        right = lax.ppermute(rows, ("row", "col"), pairs)
+        left = pick(lefts, lax.axis_index("row") ^ k)
+        out.append((left, jnp.where(lax.axis_index("row") == lax.axis_index("col"), left, right)))
     return out
 
 

time: 167 us -> 168 us (level)
  the two profiles are of different devices: /device:TPU:401 before, /device:TPU:16 now
where the time goes in v2:
time: 168 us; the launch traced here: 167 us
  starting transfers between devices  71.7 us (43%)
  waiting for transfers between devices  63.2 us (38%)
  blocking collectives  16.2 us (10%)
  matrix products  13 us (8%)
    ppermute x8, waiting for transfers between devices, direct_parts(): right = lax.ppermute(rows, ('row', 'col'), pairs)  43 us
    ppermute x8, starting transfers between devices, direct_parts(): right = lax.ppermute(rows, ('row', 'col'), pairs)  33.5 us
    ppermute x3, starting transfers between devices, reach(): lax.ppermute(rows, 'expert', [(e, e ^ d * CHIPS) for e in range(SEGMENTS...  21.9 us
    ppermute x6, starting transfers between devices, swap(): return lax.ppermute(rows, axis, [(i, i ^ mask) for i in range(SIDE)])  16.2 us
    all_to_all x1, blocking collectives, per_device(): lax.all_to_all(outgoing.reshape(CHIPS, -1, width), 'expert', 0, 0, tiled=...  16.2 us
    ppermute x3, waiting for transfers between devices, reach(): lax.ppermute(rows, 'expert', [(e, e ^ d * CHIPS) for e in range(SEGMENTS...  15.2 us
    dot_general x8, matrix products, per_device(): lax.dot_general(left, right, (((0,), (0,)), ((), ())), preferred_element_...  11.7 us
    ppermute x6, waiting for transfers between devices, swap(): return lax.ppermute(rows, axis, [(i, i ^ mask) for i in range(SIDE)])  5.02 us
  transfers between devices with their start and end apart: 17, of which 7 were waited for; matrix products, arithmetic and copies ran while one was open for 5% of the time, Pallas kernels for 0%

profile of v2, /device:TPU:16, one launch (start us, length us, event | category | flops | bytes accessed | tf_op | source)
XLA Modules:
  0.0 167.2 jit_solution(11908599269966522217)
XLA Ops:
  0.0 0.8 fusion.79
  0.9 0.8 convolution_convert_fusion.1
  1.7 0.1 copy.5
  1.8 0.1 eq.98
  1.9 0.0 copy-start.1
  2.0 0.4 convolution_convert_fusion
  2.4 16.2 %all_to_all.5 = bf16[8,48,896]{2,1,0:T(8,128)(2,1)S(1)} all-to-all(bf16[8,48,896]{2,1,0:T(8,128)(2,1)S(1)} %bitcast.11), channel_id=1, replica_groups={{0,16,32,48,64,80,96,112},{128,144,160,176,192,208,224,240},{256,272,28..., dimensions={0} | all-to-all | bytes 1376256 | tf_op jit(solution)/shard_map/all_to_all | solution.py:60
  18.6 0.1 fusion.83
  18.8 9.1 %collective-permute-start = (bf16[96,896]{1,0:T(8,128)(2,1)S(1)}, bf16[96,896]{1,0:T(8,128)(2,1)S(1)}, u32[]{:S(2)}, u32[]{:S(2)}) collective-permute-start(bf16[96,896]{1,0:T(8,128)(2,1)S(1)} %reshape.48), channel_id=1, source_target_pairs={{0,128},{16,144},{32,160},{48,176},{64,192},{80,208},{96,224},{112... | collective-permute-start | bytes 516104 | tf_op jit(solution)/shard_map/ppermute | solution.py:53
  28.0 9.1 %collective-permute-start.8 = (bf16[96,896]{1,0:T(8,128)(2,1)S(1)}, bf16[96,896]{1,0:T(8,128)(2,1)S(1)}, u32[]{:S(2)}, u32[]{:S(2)}) collective-permute-start(bf16[96,896]{1,0:T(8,128)(2,1)S(1)} %reshape.49), channel_id=1, source_target_pairs={{0,384},{16,400},{32,416},{48,432},{64,448},{80,464},{96,480},{112... | collective-permute-start | bytes 516104 | tf_op jit(solution)/shard_map/ppermute | solution.py:53
  37.2 3.7 %collective-permute-start.9 = (bf16[96,896]{1,0:T(8,128)(2,1)S(1)}, bf16[96,896]{1,0:T(8,128)(2,1)S(1)}, u32[]{:S(2)}, u32[]{:S(2)}) collective-permute-start(bf16[96,896]{1,0:T(8,128)(2,1)S(1)} %reshape.50), channel_id=1, source_target_pairs={{0,256},{16,272},{32,288},{48,304},{64,320},{80,336},{96,352},{112... | collective-permute-start | bytes 516104 | tf_op jit(solution)/shard_map/ppermute | solution.py:53
  40.9 2.4 %collective-permute-done = bf16[96,896]{1,0:T(8,128)(2,1)S(1)} collective-permute-done((bf16[96,896]{1,0:T(8,128)(2,1)S(1)}, bf16[96,896]{1,0:T(8,128)(2,1)S(1)}, u32[]{:S(2)}, u32[]{:S(2)}) %collective-permute-start) | collective-permute-done | bytes 172064 | tf_op jit(solution)/shard_map/ppermute | solution.py:53
  43.4 2.4 %collective-permute-start.1 = (bf16[192,896]{1,0:T(8,128)(2,1)S(1)}, bf16[192,896]{1,0:T(8,128)(2,1)S(1)}, u32[]{:S(2)}, u32[]{:S(2)}) collective-permute-start(bf16[192,896]{1,0:T(8,128)(2,1)S(1)} %constant_dynamic-update-slice_fusion), channel_id=1, source_target_pairs={{0,3},{1,2},{2,1},{3,0},{4,7},{5,6},{6,5},{7,4},{8,11},{9,10},{10,... | collective-permute-start | bytes 1032200 | tf_op jit(solution)/shard_map/ppermute | solution.py:12
  45.8 4.8 %collective-permute-start.2 = (bf16[192,896]{1,0:T(8,128)(2,1)S(1)}, bf16[192,896]{1,0:T(8,128)(2,1)S(1)}, u32[]{:S(2)}, u32[]{:S(2)}) collective-permute-start(bf16[192,896]{1,0:T(8,128)(2,1)S(1)} %constant_dynamic-update-slice_fusion), channel_id=1, source_target_pairs={{0,2},{1,3},{2,0},{3,1},{4,6},{5,7},{6,4},{7,5},{8,10},{9,11},{10,... | collective-permute-start | bytes 1032200 | tf_op jit(solution)/shard_map/ppermute | solution.py:12
  50.6 2.7 %collective-permute-start.3 = (bf16[192,896]{1,0:T(8,128)(2,1)S(1)}, bf16[192,896]{1,0:T(8,128)(2,1)S(1)}, u32[]{:S(2)}, u32[]{:S(2)}) collective-permute-start(bf16[192,896]{1,0:T(8,128)(2,1)S(1)} %constant_dynamic-update-slice_fusion), channel_id=1, source_target_pairs={{0,1},{1,0},{2,3},{3,2},{4,5},{5,4},{6,7},{7,6},{8,9},{9,8},{10,11... | collective-permute-start | bytes 1032200 | tf_op jit(solution)/shard_map/ppermute | solution.py:12
  53.2 12.8 %collective-permute-done.8 = bf16[96,896]{1,0:T(8,128)(2,1)S(1)} collective-permute-done((bf16[96,896]{1,0:T(8,128)(2,1)S(1)}, bf16[96,896]{1,0:T(8,128)(2,1)S(1)}, u32[]{:S(2)}, u32[]{:S(2)}) %collective-permute-start.8) | collective-permute-done | bytes 172064 | tf_op jit(solution)/shard_map/ppermute | solution.py:53
  66.1 5.2 %collective-permute-start.5 = (bf16[192,896]{1,0:T(8,128)(2,1)S(1)}, bf16[192,896]{1,0:T(8,128)(2,1)S(1)}, u32[]{:S(2)}, u32[]{:S(2)}) collective-permute-start(bf16[192,896]{1,0:T(8,128)(2,1)S(1)} %constant_dynamic-update-slice_fusion), channel_id=1, source_target_pairs={{0,4},{2,12},{3,8},{4,1},{6,9},{7,13},{8,14},{10,6},{11,2},{12,11}... | collective-permute-start | bytes 1032200 | tf_op jit(solution)/shard_map/ppermute | solution.py:39
  71.2 0.6 select_reduce_fusion
  72.5 0.0 collective-permute-done.9
  72.5 5.1 %collective-permute-start.4 = (bf16[192,896]{1,0:T(8,128)(2,1)S(1)}, bf16[192,896]{1,0:T(8,128)(2,1)S(1)}, u32[]{:S(2)}, u32[]{:S(2)}) collective-permute-start(bf16[192,896]{1,0:T(8,128)(2,1)S(1)} %constant_dynamic-update-slice_fusion), channel_id=1, source_target_pairs={{1,4},{2,8},{3,12},{5,1},{6,13},{7,9},{9,14},{10,2},{11,6},{13,11}... | collective-permute-start | bytes 1032200 | tf_op jit(solution)/shard_map/ppermute | solution.py:39
  77.7 0.0 collective-permute-done.1
  77.7 1.3 collective-permute-start.6
  79.0 0.0 collective-permute-done.2
  79.0 1.9 %collective-permute-start.10 = (bf16[192,896]{1,0:T(8,128)(2,1)S(1)}, bf16[192,896]{1,0:T(8,128)(2,1)S(1)}, u32[]{:S(2)}, u32[]{:S(2)}) collective-permute-start(bf16[192,896]{1,0:T(8,128)(2,1)S(1)} %constant_dynamic-update-slice_fusion.2), channel_id=1, source_target_pairs={{0,3},{1,2},{2,1},{3,0},{4,7},{5,6},{6,5},{7,4},{8,11},{9,10},{10,... | collective-permute-start | bytes 1032200 | tf_op jit(solution)/shard_map/ppermute | solution.py:12
  80.9 2.6 %collective-permute-start.11 = (bf16[192,896]{1,0:T(8,128)(2,1)S(1)}, bf16[192,896]{1,0:T(8,128)(2,1)S(1)}, u32[]{:S(2)}, u32[]{:S(2)}) collective-permute-start(bf16[192,896]{1,0:T(8,128)(2,1)S(1)} %constant_dynamic-update-slice_fusion.2), channel_id=1, source_target_pairs={{0,2},{1,3},{2,0},{3,1},{4,6},{5,7},{6,4},{7,5},{8,10},{9,11},{10,... | collective-permute-start | bytes 1032200 | tf_op jit(solution)/shard_map/ppermute | solution.py:12
  83.5 11.1 %collective-permute-done.5 = bf16[192,896]{1,0:T(8,128)(2,1)S(1)} collective-permute-done((bf16[192,896]{1,0:T(8,128)(2,1)S(1)}, bf16[192,896]{1,0:T(8,128)(2,1)S(1)}, u32[]{:S(2)}, u32[]{:S(2)}) %collective-permute-start.5) | collective-permute-done | bytes 344096 | tf_op jit(solution)/shard_map/ppermute | solution.py:39
  94.6 1.9 %collective-permute-start.12 = (bf16[192,896]{1,0:T(8,128)(2,1)S(1)}, bf16[192,896]{1,0:T(8,128)(2,1)S(1)}, u32[]{:S(2)}, u32[]{:S(2)}) collective-permute-start(bf16[192,896]{1,0:T(8,128)(2,1)S(1)} %constant_dynamic-update-slice_fusion.2), channel_id=1, source_target_pairs={{0,1},{1,0},{2,3},{3,2},{4,5},{5,4},{6,7},{7,6},{8,9},{9,8},{10,11... | collective-permute-start | bytes 1032200 | tf_op jit(solution)/shard_map/ppermute | solution.py:12
  96.6 0.7 fusion.14
  97.3 0.0 collective-permute-done.4
  97.3 1.9 %collective-permute-start.13 = (bf16[192,896]{1,0:T(8,128)(2,1)S(1)}, bf16[192,896]{1,0:T(8,128)(2,1)S(1)}, u32[]{:S(2)}, u32[]{:S(2)}) collective-permute-start(bf16[192,896]{1,0:T(8,128)(2,1)S(1)} %constant_dynamic-update-slice_fusion.2), channel_id=1, source_target_pairs={{1,4},{2,8},{3,12},{5,1},{6,13},{7,9},{9,14},{10,2},{11,6},{13,11}... | collective-permute-start | bytes 1032200 | tf_op jit(solution)/shard_map/ppermute | solution.py:39
  99.2 0.7 fusion.16
  100.0 5.0 %collective-permute-done.10 = bf16[192,896]{1,0:T(8,128)(2,1)S(1)} collective-permute-done((bf16[192,896]{1,0:T(8,128)(2,1)S(1)}, bf16[192,896]{1,0:T(8,128)(2,1)S(1)}, u32[]{:S(2)}, u32[]{:S(2)}) %collective-permute-start.10) | collective-permute-done | bytes 344096 | tf_op jit(solution)/shard_map/ppermute | solution.py:12
  105.0 2.9 %collective-permute-start.7 = (bf16[192,896]{1,0:T(8,128)(2,1)S(1)}, bf16[192,896]{1,0:T(8,128)(2,1)S(1)}, u32[]{:S(2)}, u32[]{:S(2)}) collective-permute-start(bf16[192,896]{1,0:T(8,128)(2,1)S(1)} %constant_dynamic-update-slice_fusion), channel_id=1, source_target_pairs={{0,12},{1,8},{2,4},{4,9},{5,13},{6,1},{8,6},{9,2},{10,14},{12,3},{... | collective-permute-start | bytes 1032200 | tf_op jit(solution)/shard_map/ppermute | solution.py:39
  107.8 12.5 %collective-permute-start.14 = (bf16[192,896]{1,0:T(8,128)(2,1)S(1)}, bf16[192,896]{1,0:T(8,128)(2,1)S(1)}, u32[]{:S(2)}, u32[]{:S(2)}) collective-permute-start(bf16[192,896]{1,0:T(8,128)(2,1)S(1)} %constant_dynamic-update-slice_fusion.2), channel_id=1, source_target_pairs={{0,4},{2,12},{3,8},{4,1},{6,9},{7,13},{8,14},{10,6},{11,2},{12,11}... | collective-permute-start | bytes 1032200 | tf_op jit(solution)/shard_map/ppermute | solution.py:39
  120.3 0.0 collective-permute-done.12
  120.3 1.3 collective-permute-start.15
  121.6 0.0 collective-permute-done.13
  121.6 3.4 %collective-permute-start.16 = (bf16[192,896]{1,0:T(8,128)(2,1)S(1)}, bf16[192,896]{1,0:T(8,128)(2,1)S(1)}, u32[]{:S(2)}, u32[]{:S(2)}) collective-permute-start(bf16[192,896]{1,0:T(8,128)(2,1)S(1)} %constant_dynamic-update-slice_fusion.2), channel_id=1, source_target_pairs={{0,12},{1,8},{2,4},{4,9},{5,13},{6,1},{8,6},{9,2},{10,14},{12,3},{... | collective-permute-start | bytes 1032200 | tf_op jit(solution)/shard_map/ppermute | solution.py:39
  125.1 0.7 fusion.8
  125.8 8.9 %collective-permute-done.14 = bf16[192,896]{1,0:T(8,128)(2,1)S(1)} collective-permute-done((bf16[192,896]{1,0:T(8,128)(2,1)S(1)}, bf16[192,896]{1,0:T(8,128)(2,1)S(1)}, u32[]{:S(2)}, u32[]{:S(2)}) %collective-permute-start.14) | collective-permute-done | bytes 344096 | tf_op jit(solution)/shard_map/ppermute | solution.py:39
  134.7 0.7 fusion.6
  135.4 0.0 collective-permute-done.6
  135.4 0.7 fusion.12
  136.1 21.3 %collective-permute-done.15 = bf16[192,896]{1,0:T(8,128)(2,1)S(1)} collective-permute-done((bf16[192,896]{1,0:T(8,128)(2,1)S(1)}, bf16[192,896]{1,0:T(8,128)(2,1)S(1)}, u32[]{:S(2)}, u32[]{:S(2)}) %collective-permute-start.15) | collective-permute-done | bytes 344096 | tf_op jit(solution)/shard_map/ppermute | solution.py:39
  157.5 0.7 fusion.4
  158.2 2.4 %fusion.10 = f32[896,896]{1,0:T(8,128)} fusion(bf16[192,896]{1,0:T(8,128)(2,1)S(1)} %collective-permute-done.7, bf16[192,896]{1,0:T(8,128)(2,1)S(1)} %collective-permute-done.1, bf16[192,896]{1,0:T(8,128)(2,1)S(1)} %collective-permute-done.2, bf16[192,896]{1,0:T(8,128)(2,1)S(1)} %collective-permute-done.3, ...), kind=kOutput, calls=%fused_computation.11 | convolution fusion | flops 309485568 | bytes 4931588 | tf_op jit(solution)/shard_map/dot_general | solution.py:68
  160.6 1.6 collective-permute-done.16
  162.2 5.0 %divide_bitcast_fusion = f32[1,896,896]{2,1,0:T(8,128)} fusion(f32[896,896]{1,0:T(8,128)S(1)} %fusion.4, f32[896,896]{1,0:T(8,128)S(1)} %fusion.6, f32[896,896]{1,0:T(8,128)S(1)} %fusion.8, f32[896,896]{1,0:T(8,128)} %fusion.10, f32[896,896]{1,0:T(8,128)S(1)} %fusion.12, f32[896,896]{1,0:T(8,128)S(1)} %fusion.16, f32[896,896]{1,0:T(8,128)S(1)} %fusion.14, ...), kind=kOutput, calls=%fused_computation | convolution fusion | flops 315908096 | bytes 27410440 | tf_op jit(solution)/shard_map/dot_general | solution.py:68
  (20 shorter events, 0.3 us)
Async XLA Ops:
  0.0 1.9 %copy-start = (bf16[256,896]{1,0:T(8,128)(2,1)S(1)}, bf16[256,896]{1,0:T(8,128)(2,1)}, u32[]{:S(2)}) copy-start(bf16[256,896]{1,0:T(8,128)(2,1)} %param.4) | copy-start | bytes 1376260
  0.0 27.9 %copy-start.2 = (s32[32]{0:T(128)S(1)}, s32[32]{0:T(128)}, u32[]{:S(2)}) copy-start(s32[32]{0:T(128)} %param.7) | copy-start | bytes 388
  1.9 69.3 %copy-start.1 = (s32[6,32]{1,0:T(8,128)S(1)}, s32[6,32]{1,0:T(8,128)}, u32[]{:S(2)}) copy-start(s32[6,32]{1,0:T(8,128)} %param.6) | copy-start | bytes 2308
  18.8 24.6 %collective-permute-start = (bf16[96,896]{1,0:T(8,128)(2,1)S(1)}, bf16[96,896]{1,0:T(8,128)(2,1)S(1)}, u32[]{:S(2)}, u32[]{:S(2)}) collective-permute-start(bf16[96,896]{1,0:T(8,128)(2,1)S(1)} %reshape.48), channel_id=1, source_target_pairs={{0,128},{16,144},{32,160},{48,176},{64,192},{80,208},{96,224},{112... | collective-permute-start | bytes 516104 | tf_op jit(solution)/shard_map/ppermute | solution.py:53
  28.0 38.0 %collective-permute-start.8 = (bf16[96,896]{1,0:T(8,128)(2,1)S(1)}, bf16[96,896]{1,0:T(8,128)(2,1)S(1)}, u32[]{:S(2)}, u32[]{:S(2)}) collective-permute-start(bf16[96,896]{1,0:T(8,128)(2,1)S(1)} %reshape.49), channel_id=1, source_target_pairs={{0,384},{16,400},{32,416},{48,432},{64,448},{80,464},{96,480},{112... | collective-permute-start | bytes 516104 | tf_op jit(solution)/shard_map/ppermute | solution.py:53
  37.2 35.3 %collective-permute-start.9 = (bf16[96,896]{1,0:T(8,128)(2,1)S(1)}, bf16[96,896]{1,0:T(8,128)(2,1)S(1)}, u32[]{:S(2)}, u32[]{:S(2)}) collective-permute-start(bf16[96,896]{1,0:T(8,128)(2,1)S(1)} %reshape.50), channel_id=1, source_target_pairs={{0,256},{16,272},{32,288},{48,304},{64,320},{80,336},{96,352},{112... | collective-permute-start | bytes 516104 | tf_op jit(solution)/shard_map/ppermute | solution.py:53
  43.4 34.3 %collective-permute-start.1 = (bf16[192,896]{1,0:T(8,128)(2,1)S(1)}, bf16[192,896]{1,0:T(8,128)(2,1)S(1)}, u32[]{:S(2)}, u32[]{:S(2)}) collective-permute-start(bf16[192,896]{1,0:T(8,128)(2,1)S(1)} %constant_dynamic-update-slice_fusion), channel_id=1, source_target_pairs={{0,3},{1,2},{2,1},{3,0},{4,7},{5,6},{6,5},{7,4},{8,11},{9,10},{10,... | collective-permute-start | bytes 1032200 | tf_op jit(solution)/shard_map/ppermute | solution.py:12
  45.8 33.2 %collective-permute-start.2 = (bf16[192,896]{1,0:T(8,128)(2,1)S(1)}, bf16[192,896]{1,0:T(8,128)(2,1)S(1)}, u32[]{:S(2)}, u32[]{:S(2)}) collective-permute-start(bf16[192,896]{1,0:T(8,128)(2,1)S(1)} %constant_dynamic-update-slice_fusion), channel_id=1, source_target_pairs={{0,2},{1,3},{2,0},{3,1},{4,6},{5,7},{6,4},{7,5},{8,10},{9,11},{10,... | collective-permute-start | bytes 1032200 | tf_op jit(solution)/shard_map/ppermute | solution.py:12
  50.6 30.3 %collective-permute-start.3 = (bf16[192,896]{1,0:T(8,128)(2,1)S(1)}, bf16[192,896]{1,0:T(8,128)(2,1)S(1)}, u32[]{:S(2)}, u32[]{:S(2)}) collective-permute-start(bf16[192,896]{1,0:T(8,128)(2,1)S(1)} %constant_dynamic-update-slice_fusion), channel_id=1, source_target_pairs={{0,1},{1,0},{2,3},{3,2},{4,5},{5,4},{6,7},{7,6},{8,9},{9,8},{10,11... | collective-permute-start | bytes 1032200 | tf_op jit(solution)/shard_map/ppermute | solution.py:12
  66.1 28.6 %collective-permute-start.5 = (bf16[192,896]{1,0:T(8,128)(2,1)S(1)}, bf16[192,896]{1,0:T(8,128)(2,1)S(1)}, u32[]{:S(2)}, u32[]{:S(2)}) collective-permute-start(bf16[192,896]{1,0:T(8,128)(2,1)S(1)} %constant_dynamic-update-slice_fusion), channel_id=1, source_target_pairs={{0,4},{2,12},{3,8},{4,1},{6,9},{7,13},{8,14},{10,6},{11,2},{12,11}... | collective-permute-start | bytes 1032200 | tf_op jit(solution)/shard_map/ppermute | solution.py:39
  72.5 24.7 %collective-permute-start.4 = (bf16[192,896]{1,0:T(8,128)(2,1)S(1)}, bf16[192,896]{1,0:T(8,128)(2,1)S(1)}, u32[]{:S(2)}, u32[]{:S(2)}) collective-permute-start(bf16[192,896]{1,0:T(8,128)(2,1)S(1)} %constant_dynamic-update-slice_fusion), channel_id=1, source_target_pairs={{1,4},{2,8},{3,12},{5,1},{6,13},{7,9},{9,14},{10,2},{11,6},{13,11}... | collective-permute-start | bytes 1032200 | tf_op jit(solution)/shard_map/ppermute | solution.py:39
  77.7 57.7 %collective-permute-start.6 = (bf16[192,896]{1,0:T(8,128)(2,1)S(1)}, bf16[192,896]{1,0:T(8,128)(2,1)S(1)}, u32[]{:S(2)}, u32[]{:S(2)}) collective-permute-start(bf16[192,896]{1,0:T(8,128)(2,1)S(1)} %constant_dynamic-update-slice_fusion), channel_id=1, source_target_pairs={{0,8},{1,12},{3,4},{4,13},{5,9},{7,1},{8,2},{9,6},{11,14},{12,7},{... | collective-permute-start | bytes 1032200 | tf_op jit(solution)/shard_map/ppermute | solution.py:39
  79.0 26.0 %collective-permute-start.10 = (bf16[192,896]{1,0:T(8,128)(2,1)S(1)}, bf16[192,896]{1,0:T(8,128)(2,1)S(1)}, u32[]{:S(2)}, u32[]{:S(2)}) collective-permute-start(bf16[192,896]{1,0:T(8,128)(2,1)S(1)} %constant_dynamic-update-slice_fusion.2), channel_id=1, source_target_pairs={{0,3},{1,2},{2,1},{3,0},{4,7},{5,6},{6,5},{7,4},{8,11},{9,10},{10,... | collective-permute-start | bytes 1032200 | tf_op jit(solution)/shard_map/ppermute | solution.py:12
  80.9 26.9 %collective-permute-start.11 = (bf16[192,896]{1,0:T(8,128)(2,1)S(1)}, bf16[192,896]{1,0:T(8,128)(2,1)S(1)}, u32[]{:S(2)}, u32[]{:S(2)}) collective-permute-start(bf16[192,896]{1,0:T(8,128)(2,1)S(1)} %constant_dynamic-update-slice_fusion.2), channel_id=1, source_target_pairs={{0,2},{1,3},{2,0},{3,1},{4,6},{5,7},{6,4},{7,5},{8,10},{9,11},{10,... | collective-permute-start | bytes 1032200 | tf_op jit(solution)/shard_map/ppermute | solution.py:12
  94.6 25.7 %collective-permute-start.12 = (bf16[192,896]{1,0:T(8,128)(2,1)S(1)}, bf16[192,896]{1,0:T(8,128)(2,1)S(1)}, u32[]{:S(2)}, u32[]{:S(2)}) collective-permute-start(bf16[192,896]{1,0:T(8,128)(2,1)S(1)} %constant_dynamic-update-slice_fusion.2), channel_id=1, source_target_pairs={{0,1},{1,0},{2,3},{3,2},{4,5},{5,4},{6,7},{7,6},{8,9},{9,8},{10,11... | collective-permute-start | bytes 1032200 | tf_op jit(solution)/shard_map/ppermute | solution.py:12
  97.3 24.3 %collective-permute-start.13 = (bf16[192,896]{1,0:T(8,128)(2,1)S(1)}, bf16[192,896]{1,0:T(8,128)(2,1)S(1)}, u32[]{:S(2)}, u32[]{:S(2)}) collective-permute-start(bf16[192,896]{1,0:T(8,128)(2,1)S(1)} %constant_dynamic-update-slice_fusion.2), channel_id=1, source_target_pairs={{1,4},{2,8},{3,12},{5,1},{6,13},{7,9},{9,14},{10,2},{11,6},{13,11}... | collective-permute-start | bytes 1032200 | tf_op jit(solution)/shard_map/ppermute | solution.py:39
  105.0 53.3 %collective-permute-start.7 = (bf16[192,896]{1,0:T(8,128)(2,1)S(1)}, bf16[192,896]{1,0:T(8,128)(2,1)S(1)}, u32[]{:S(2)}, u32[]{:S(2)}) collective-permute-start(bf16[192,896]{1,0:T(8,128)(2,1)S(1)} %constant_dynamic-update-slice_fusion), channel_id=1, source_target_pairs={{0,12},{1,8},{2,4},{4,9},{5,13},{6,1},{8,6},{9,2},{10,14},{12,3},{... | collective-permute-start | bytes 1032200 | tf_op jit(solution)/shard_map/ppermute | solution.py:39
  107.8 26.9 %collective-permute-start.14 = (bf16[192,896]{1,0:T(8,128)(2,1)S(1)}, bf16[192,896]{1,0:T(8,128)(2,1)S(1)}, u32[]{:S(2)}, u32[]{:S(2)}) collective-permute-start(bf16[192,896]{1,0:T(8,128)(2,1)S(1)} %constant_dynamic-update-slice_fusion.2), channel_id=1, source_target_pairs={{0,4},{2,12},{3,8},{4,1},{6,9},{7,13},{8,14},{10,6},{11,2},{12,11}... | collective-permute-start | bytes 1032200 | tf_op jit(solution)/shard_map/ppermute | solution.py:39
  120.3 37.2 %collective-permute-start.15 = (bf16[192,896]{1,0:T(8,128)(2,1)S(1)}, bf16[192,896]{1,0:T(8,128)(2,1)S(1)}, u32[]{:S(2)}, u32[]{:S(2)}) collective-permute-start(bf16[192,896]{1,0:T(8,128)(2,1)S(1)} %constant_dynamic-update-slice_fusion.2), channel_id=1, source_target_pairs={{0,8},{1,12},{3,4},{4,13},{5,9},{7,1},{8,2},{9,6},{11,14},{12,7},{... | collective-permute-start | bytes 1032200 | tf_op jit(solution)/shard_map/ppermute | solution.py:39
  121.6 40.6 %collective-permute-start.16 = (bf16[192,896]{1,0:T(8,128)(2,1)S(1)}, bf16[192,896]{1,0:T(8,128)(2,1)S(1)}, u32[]{:S(2)}, u32[]{:S(2)}) collective-permute-start(bf16[192,896]{1,0:T(8,128)(2,1)S(1)} %constant_dynamic-update-slice_fusion.2), channel_id=1, source_target_pairs={{0,12},{1,8},{2,4},{4,9},{5,13},{6,1},{8,6},{9,2},{10,14},{12,3},{... | collective-permute-start | bytes 1032200 | tf_op jit(solution)/shard_map/ppermute | solution.py:39
